TPU v7x, 256 devices: a whole 4x4x8 slice. The times are simulated.
256 devices in a mesh: dom: 64 (over z, x, core), rep: 4 (over y).
Axes of the slice: x: 4, y: 4, z: 8, core: 2. Of those that a mesh axis runs over, the one named last changes fastest.
Arguments:
- entities: bfloat16 [65536, 512], P('dom'), may hold values from -60 to 60
- relations: bfloat16 [4, 512, 512], replicated, may hold values from -2 to 2
- head_local: int32 [131072], P(('dom', 'rep')), may hold values from 0 to 1023
- rel_ids: int32 [131072], P(('dom', 'rep')), may hold values from 0 to 3
- tail_part: int32 [131072, 1], P(('dom', 'rep')), may hold values from 0 to 63; in each aligned block of 512 rows (0 to 511, 512 to 1023, ...) at most 16 rows name the same one
- tail_local: int32 [131072], P(('dom', 'rep')), may hold values from 0 to 1023
- neg_local: int32 [2048], P('dom'), may hold values from 0 to 1023
Outputs:
- entity_grad: float32 [65536, 512], P('dom')
- relation_grad: float32 [4, 512, 512], replicated
- edge_loss: float32 [131072], P(('dom', 'rep'))
Inputs may be any that keep to these rules, and one draw needn't show every extreme that they name: `tail_part`: in the 512 edges of one device no partition is named by more than 16 edges, a bound that some block reaches.
All inputs are finite; a program needn't handle non-finite values.
Results may differ from a plain program's by a relative error of at most 0.012.
The roundings to bfloat16 on the way count: a program that leaves them out, or rounds other values in their place, can miss the bound.
Values may be sent and summed in bfloat16 or wider, within the bound.
A program may use at most 64 MiB of HBM per device.

v0:
```python
import math

import jax
import jax.numpy as jnp
from jax import lax
from jax.sharding import PartitionSpec as P

D = 512


def local(entities, relations, head_local, rel_ids, tail_part, tail_local, neg_local):
    factor = 1.0 / math.sqrt(D)
    ent_dev = entities.shape[0]
    columns = entities.shape[1]
    edge_count = head_local.shape[0]
    part_count = lax.axis_size("dom")
    capacity = 2 * edge_count // part_count
    slot_count = part_count * capacity
    relation_count = relations.shape[0]
    head_rows = jnp.take(entities, head_local, axis=0)
    selectors = [(rel_ids == relation)[:, None] for relation in range(relation_count)]
    query_sum = jnp.zeros((edge_count, columns), jnp.float32)
    for relation in range(relation_count):
        picked = jnp.where(selectors[relation], head_rows, jnp.zeros_like(head_rows))
        query_sum = query_sum + jnp.dot(
            picked, relations[relation], preferred_element_type=jnp.float32
        )
    queries = query_sum.astype(jnp.bfloat16)
    target = tail_part[:, 0]
    target_hot = (target[:, None] == jnp.arange(part_count, dtype=jnp.int32)[None, :]).astype(
        jnp.int32
    )
    earlier = jnp.cumsum(target_hot, axis=0) - target_hot
    position = jnp.sum(earlier * target_hot, axis=1)
    slot_index = target * capacity + position
    slot_match = (slot_index[None, :] == jnp.arange(slot_count, dtype=jnp.int32)[:, None]).astype(
        jnp.int32
    )
    filled = jnp.sum(slot_match, axis=1) > 0
    source = jnp.sum(slot_match * jnp.arange(edge_count, dtype=jnp.int32)[None, :], axis=1)
    send_ids = jnp.where(filled, jnp.take(tail_local, source, axis=0), 0).reshape(
        part_count, capacity
    )
    recv_ids = lax.all_to_all(send_ids, "dom", split_axis=0, concat_axis=0, tiled=True)
    looked_up = jnp.take(entities, recv_ids.reshape(-1), axis=0).reshape(
        part_count, capacity, columns
    )
    returned = lax.all_to_all(looked_up, "dom", split_axis=0, concat_axis=0, tiled=True)
    tail_embed = jnp.take(returned.reshape(slot_count, columns), slot_index, axis=0)
    own_negs = jnp.take(entities, neg_local, axis=0)
    negatives = lax.all_gather(own_negs, "dom", axis=0, tiled=True)
    positive = (
        jnp.sum(queries.astype(jnp.float32) * tail_embed.astype(jnp.float32), axis=1) * factor
    )
    scores = (
        lax.dot_general(
            queries, negatives, (((1,), (1,)), ((), ())), preferred_element_type=jnp.float32
        )
        * factor
    )
    row_max = jnp.maximum(positive, jnp.max(scores, axis=1))
    exp_pos = jnp.exp(positive - row_max)
    exp_neg = jnp.exp(scores - row_max[:, None])
    partition_sum = exp_pos + jnp.sum(exp_neg, axis=1)
    edge_loss = jnp.log(partition_sum) + row_max - positive
    prob_pos = exp_pos / partition_sum
    prob_neg = (exp_neg / partition_sum[:, None]).astype(jnp.bfloat16)
    mixed = jnp.dot(prob_neg, negatives, preferred_element_type=jnp.float32)
    query_grad = (
        factor * ((prob_pos - 1.0)[:, None] * tail_embed.astype(jnp.float32) + mixed)
    ).astype(jnp.bfloat16)
    tail_grad = factor * (prob_pos - 1.0)[:, None] * queries.astype(jnp.float32)
    neg_grad = factor * lax.dot_general(
        prob_neg, queries, (((0,), (0,)), ((), ())), preferred_element_type=jnp.float32
    )
    head_grad = jnp.zeros((edge_count, columns), jnp.float32)
    rel_terms = []
    for relation in range(relation_count):
        picked_grad = jnp.where(selectors[relation], query_grad, jnp.zeros_like(query_grad))
        head_grad = head_grad + lax.dot_general(
            picked_grad,
            relations[relation],
            (((1,), (1,)), ((), ())),
            preferred_element_type=jnp.float32,
        )
        picked_rows = jnp.where(selectors[relation], head_rows, jnp.zeros_like(head_rows))
        rel_terms.append(
            lax.dot_general(
                picked_rows,
                query_grad,
                (((0,), (0,)), ((), ())),
                preferred_element_type=jnp.float32,
            )
        )
    relation_grad = lax.psum(jnp.stack(rel_terms), ("dom", "rep"))
    grad_send = jnp.where(filled[:, None], jnp.take(tail_grad, source, axis=0), 0.0)
    grad_recv = lax.all_to_all(
        grad_send.reshape(part_count, capacity, columns),
        "dom",
        split_axis=0,
        concat_axis=0,
        tiled=True,
    )
    owned = lax.psum_scatter(neg_grad, "dom", scatter_dimension=0, tiled=True)
    target_ids = jnp.concatenate([head_local, recv_ids.reshape(-1), neg_local])
    target_rows = jnp.concatenate(
        [head_grad, grad_recv.reshape(slot_count, columns), owned], axis=0
    )
    block_rows = min(512, ent_dev)
    block_count = ent_dev // block_rows

    def add_block(start):
        hot = (
            target_ids[None, :] == (start + jnp.arange(block_rows, dtype=jnp.int32))[:, None]
        ).astype(jnp.float32)
        return jnp.dot(
            hot, target_rows, precision=lax.Precision.HIGHEST, preferred_element_type=jnp.float32
        )

    local_grad = lax.map(add_block, jnp.arange(block_count, dtype=jnp.int32) * block_rows).reshape(
        ent_dev, columns
    )
    entity_grad = lax.psum(local_grad, "rep")
    return (entity_grad, relation_grad, edge_loss)


def solution(mesh):
    return jax.shard_map(
        local,
        mesh=mesh,
        in_specs=(
            P("dom", None),
            P(),
            P(("dom", "rep")),
            P(("dom", "rep")),
            P(("dom", "rep"), None),
            P(("dom", "rep")),
            P("dom"),
        ),
        out_specs=(P("dom", None), P(), P(("dom", "rep"))),
        check_vma=False,
    )
```

profile of v0, /device:TPU:1, one launch (start us, length us, event | category | flops | bytes accessed | tf_op | source)
XLA Modules:
  0.0 596.3 jit_solution(15604910715601647900)
XLA Ops:
  7.2 0.7 compare_select_fusion.7
  8.0 0.7 compare_and_fusion.4
  8.7 0.6 gather_fusion.2
  9.3 0.7 broadcast_select_fusion.23
  10.0 0.7 fusion.56
  10.7 1.2 reduce-window.6
  11.9 0.2 slice_reduce_fusion
  12.2 0.8 fusion.55
  13.0 0.7 compare_and_fusion.2
  13.7 0.7 select_reduce_fusion
  14.5 6.9 %gather_fusion = s32[1024]{0:T(1024)S(1)} fusion(s32[512]{0:T(512)S(1)} %copy-done.1, s32[1024]{0:T(1024)S(1)} %broadcast_clamp_fusion.1), kind=kCustom, calls=%fused_computation.2 | custom fusion | bytes 12288 | tf_op jit(solution)/shard_map/jit(_take)/gather | solution.py:41
  21.5 22.2 %all_to_all.16 = s32[64,1,16]{2,1,0:T(1,128)S(1)} all-to-all(s32[64,1,16]{2,1,0:T(1,128)S(1)} %bitcast.90), channel_id=1, replica_groups=mesh['dom'=64,'rep'=4] {'dom'}, dimensions={0} | all-to-all | bytes 8192 | tf_op jit(solution)/shard_map/all_to_all | solution.py:44
  43.8 4.0 gather_fusion.1
  47.8 1.2 broadcast_select_fusion
  49.0 4.8 all-to-all-start.1
  53.8 0.2 reduce-scatter.2.cloned.1.call-start
  54.0 2.0 gather_fusion.4
  56.0 0.2 copy.27
  56.3 1.7 fusion.23
  58.2 0.5 convolution_add_fusion.5
  58.7 1.5 convolution_add_fusion.4
  60.1 24.6 %all-to-all-done.1 = bf16[64,16,512]{2,1,0:T(8,128)(2,1)S(1)} async-done(((bf16[64,16,512]{2,1,0:T(8,128)(2,1)}), bf16[64,16,512]{2,1,0:T(8,128)(2,1)S(1)}, u32[]{:S(2)}, u32[]{:S(2)}) %all-to-all-start.1) | async-done | bytes 1048608 | tf_op jit(solution)/shard_map/all_to_all | solution.py:48
  84.7 2.0 gather_fusion.5
  86.7 0.2 copy.28
  86.9 2.1 fusion.14
  89.0 5.9 all-gather.2.cloned.1.call-done
  94.9 3.0 multiply_reduce_fusion
  97.9 0.8 fusion.10
  98.7 0.6 broadcast_multiply_fusion
  99.3 0.8 divide_convert_fusion
  100.2 1.3 copy-done.2
  101.5 3.3 convolution_multiply_fusion
  105.1 0.3 copy.30
  105.5 4.9 gather_fusion.3
  110.3 2.7 select_select_fusion
  113.1 6.7 %all-to-all-start.2 = ((f32[64,16,512]{2,1,0:T(8,128)}), f32[64,16,512]{2,1,0:T(8,128)}, u32[]{:S(2)}, u32[]{:S(2)}) async-start(f32[64,16,512]{2,1,0:T(8,128)} %select_select_fusion), calls=%async_computation.2 | async-start | bytes 4194304 | tf_op jit(solution)/shard_map/all_to_all | solution.py:97
  119.8 0.3 all-reduce.5.cloned.1.call-start
  120.1 0.5 broadcast.287
  120.6 0.7 reduce.7
  121.4 3.1 fusion.12
  124.5 0.5 convolution_bitcast_fusion
  125.0 0.5 convolution_bitcast_fusion.1
  125.5 0.5 convolution_bitcast_fusion.2
  125.9 0.5 convolution_bitcast_fusion.3
  126.4 2.4 pad_maximum_fusion
  128.9 1.0 copy-done.7
  129.9 1.7 fusion.21
  131.7 0.5 convolution_add_fusion.2
  132.2 0.5 convolution_add_fusion.1
  132.7 0.5 convolution_add_fusion
  133.2 36.2 %all-to-all-done.2 = f32[64,16,512]{2,1,0:T(8,128)} async-done(((f32[64,16,512]{2,1,0:T(8,128)}), f32[64,16,512]{2,1,0:T(8,128)}, u32[]{:S(2)}, u32[]{:S(2)}) %all-to-all-start.2) | async-done | bytes 2097184 | tf_op jit(solution)/shard_map/all_to_all | solution.py:97
  169.4 71.1 %reduce-scatter.2.cloned.1.call-done = f32[32,512]{1,0:T(8,128)} async-done(((f32[2048,512]{1,0:T(8,128)}), f32[32,512]{1,0:T(8,128)}) %reduce-scatter.2.cloned.1.call-update) | async-done | bytes 65552 | tf_op jit(solution)/shard_map/reduce_scatter | solution.py:104
  240.4 3.6 pad_maximum_fusion.1
  244.1 14.5 %while.10 = (s32[]{:T(128)}, f32[2,512,512]{2,1,0:T(8,128)}, s32[1568]{0:T(1024)S(1)}, s32[2]{0:T(128)S(1)}, f32[1568,512]{1,0:T(8,128)}, /*index=5*/s32[]{:T(128)}) while((s32[]{:T(128)}, f32[2,512,512]{2,1,0:T(8,128)}, s32[1568]{0:T(1024)S(1)}, s32[2]{0:T(128)S(1)}, f32[1568,512]{1,0:T(8,128)}, /*index=5*/s32[]{:T(128)}) %tuple.34), condition=%wide.region_10.12_spmd, body=%wide.region_9.11_spmd.sunk | while | flops 4933304832 | bytes 4270305 | solution.py:120
  244.1 0.6 dynamic_slice.5
  244.6 0.6 iota_add_fusion.2
  245.2 6.1 %fusion.94 = f32[2,512,512]{2,1,0:T(8,128)} fusion(f32[2,512,512]{2,1,0:T(8,128)} %get-tuple-element.97, s32[]{:T(128)S(6)} %copy.37, f32[1568,512]{1,0:T(8,128)} %get-tuple-element.106, s32[1568]{0:T(1024)S(1)} %get-tuple-element.104, s32[512]{0:T(512)S(1)} %iota_add_fusion.2), kind=kOutput, calls=%fused_computation.11.clone.1 | convolution fusion | flops 4933304320 | bytes 4268164 | tf_op jit(solution)/shard_map/while/body/eval_jaxpr/dot_general | solution.py:116
  251.3 0.6 dynamic_slice.5
  251.9 0.6 iota_add_fusion.2
  252.5 6.1 %fusion.94 = f32[2,512,512]{2,1,0:T(8,128)} fusion(f32[2,512,512]{2,1,0:T(8,128)} %get-tuple-element.97, s32[]{:T(128)S(6)} %copy.37, f32[1568,512]{1,0:T(8,128)} %get-tuple-element.106, s32[1568]{0:T(1024)S(1)} %get-tuple-element.104, s32[512]{0:T(512)S(1)} %iota_add_fusion.2), kind=kOutput, calls=%fused_computation.11.clone.1 | convolution fusion | flops 4933304320 | bytes 4268164 | tf_op jit(solution)/shard_map/while/body/eval_jaxpr/dot_general | solution.py:116
  258.6 258.9 %all-reduce.5.cloned.1.call-done = f32[4,512,512]{2,1,0:T(8,128)} async-done(((f32[4,512,512]{2,1,0:T(8,128)}), f32[4,512,512]{2,1,0:T(8,128)}) %all-reduce.5.cloned.1.call-update) | async-done | bytes 4194320 | tf_op jit(solution)/shard_map/psum | solution.py:95
  517.5 67.0 %all-reduce.3.cloned.1.call-done = f32[1024,512]{1,0:T(8,128)} async-done(((f32[1024,512]{1,0:T(8,128)}), f32[1024,512]{1,0:T(8,128)}) %all-reduce.3.cloned.1.call-update) | async-done | bytes 2097168 | tf_op jit(solution)/shard_map/psum | solution.py:123
  584.5 3.2 copy.45
  587.7 2.0 copy.46
  (62 shorter events, 1.3 us)
Async XLA Ops:
  7.2 1.5 copy-start
  7.2 7.4 %copy-start.1 = (s32[512]{0:T(512)S(1)}, s32[512]{0:T(512)}, u32[]{:S(2)}) copy-start(s32[512]{0:T(512)} %param.16) | copy-start | bytes 6148
  7.2 87.7 %all-gather.2.cloned.1.call-start = ((), (), s32[]{:S(2)}) async-start(), calls=%async_computation.4 | async-start | bytes 2129920 | tf_op jit(solution)/shard_map/all_gather | solution.py:51
  47.8 6.2 %copy-start.12 = (s32[512]{0:T(512)S(1)}, s32[512]{0:T(512)}, u32[]{:S(2)}) copy-start(s32[512]{0:T(512)} %param.13) | copy-start | bytes 6148
  49.0 35.7 %all-to-all-start.1 = ((bf16[64,16,512]{2,1,0:T(8,128)(2,1)}), bf16[64,16,512]{2,1,0:T(8,128)(2,1)S(1)}, u32[]{:S(2)}, u32[]{:S(2)}) async-start(bf16[64,16,512]{2,1,0:T(8,128)(2,1)} %broadcast_select_fusion), calls=%async_computation.1 | async-start | bytes 2097152 | tf_op jit(solution)/shard_map/all_to_all | solution.py:48
  53.8 186.7 %reduce-scatter.2.cloned.1.call-start = ((), (), s32[]{:S(2)}) async-start(), calls=%async_computation.5 | async-start | bytes 4259840 | tf_op jit(solution)/shard_map/reduce_scatter | solution.py:104
  54.0 2.3 copy-start.13
  56.2 30.7 %copy-start.4 = (bf16[512,512]{0,1:T(8,128)(2,1)}, bf16[512,512]{0,1:T(8,128)(2,1)S(1)}, u32[]{:S(2)}) copy-start(bf16[512,512]{0,1:T(8,128)(2,1)S(1)} %copy.27) | copy-start | bytes 1572868
  56.2 1.9 copy-start.9
  86.9 2.1 copy-start.11
  100.2 1.3 copy-start.2
  113.1 8.3 %copy-start.14 = (s32[32]{0:T(128)S(1)}, s32[32]{0:T(128)}, u32[]{:S(2)}) copy-start(s32[32]{0:T(128)} %param.17) | copy-start | bytes 388
  113.1 8.3 %copy-start.3 = (bf16[512,2048]{1,0:T(8,128)(2,1)S(1)}, bf16[512,2048]{1,0:T(8,128)(2,1)}, u32[]{:S(2)}) copy-start(bf16[512,2048]{1,0:T(8,128)(2,1)} %copy-done.2) | copy-start | bytes 6291460
  113.1 56.3 %all-to-all-start.2 = ((f32[64,16,512]{2,1,0:T(8,128)}), f32[64,16,512]{2,1,0:T(8,128)}, u32[]{:S(2)}, u32[]{:S(2)}) async-start(f32[64,16,512]{2,1,0:T(8,128)} %select_select_fusion), calls=%async_computation.2 | async-start | bytes 4194304 | tf_op jit(solution)/shard_map/all_to_all | solution.py:97
  119.8 397.7 %all-reduce.5.cloned.1.call-start = ((), (), s32[]{:S(2)}) async-start(), calls=%async_computation.7 | async-start | bytes 8388608 | tf_op jit(solution)/shard_map/psum | solution.py:95
  121.4 3.1 copy-start.5
  124.5 1.4 copy-start.6
  128.8 1.1 copy-start.7
  128.9 455.6 %all-reduce.3.cloned.1.call-start = ((), (), s32[]{:S(2)}) async-start(), calls=%async_computation.6 | async-start | bytes 4194304 | tf_op jit(solution)/shard_map/psum | solution.py:123
  129.9 1.8 copy-start.10
  584.5 3.2 copy-start.8
Sparse Core Ops, SparseCore 0:
  10.8 84.0 all-gather.1
  104.9 135.4 reduce-scatter.1
  246.8 270.6 all-reduce.4
  520.3 64.1 all-reduce.2
where the time goes:
time: 597 us; the launch traced here: 596 us
  waiting for transfers between devices  464 us (78%)
  matrix products  32.5 us (5%)
  local copies, waits for them, and re-layouts  31.2 us (5%)
  blocking collectives  22.2 us (4%)
  other arithmetic  20.5 us (3%)
  between operations  14.2 us (2%)
  starting transfers between devices  12 us (2%)
    psum x1, waiting for transfers between devices, local(): relation_grad = lax.psum(jnp.stack(rel_terms), ('dom', 'rep'))  259 us
    reduce_scatter x1, waiting for transfers between devices, local(): owned = lax.psum_scatter(neg_grad, 'dom', scatter_dimension=0, tiled=True)  71.1 us
    psum x1, waiting for transfers between devices, local(): entity_grad = lax.psum(local_grad, 'rep')  67 us
    all_to_all x1, waiting for transfers between devices, local(): lax.all_to_all(grad_send.reshape(part_count, capacity, columns), 'dom', s...  36.2 us
    all_to_all x1, waiting for transfers between devices, local(): lax.all_to_all(looked_up, 'dom', split_axis=0, concat_axis=0, tiled=True)  24.6 us
    all_to_all x1, blocking collectives, local(): lax.all_to_all(send_ids, 'dom', split_axis=0, concat_axis=0, tiled=True)  22.2 us
    dot_general x2, matrix products, add_block(): jnp.dot(hot, target_rows, precision=lax.Precision.HIGHEST, preferred_elem...  12.3 us
  transfers between devices with their start and end apart: 6, of which 6 were waited for; matrix products, arithmetic and copies ran while one was open for 11% of the time, Pallas kernels for 0%

commit v1 on v0

--- a/solution.py
+++ b/solution.py
@@ -1,11 +1,182 @@
+import functools
 import math
 
 import jax
 import jax.numpy as jnp
 from jax import lax
+from jax.experimental import pallas as pl
+from jax.experimental.pallas import tpu as pltpu
 from jax.sharding import PartitionSpec as P
 
 D = 512
+
+
+def _stage(name, dom, rep, n_dom, n_rep):
+    core, xx, zz = dom % 2, (dom // 2) % 4, dom // 8
+    if name == "core":
+        return 2, core, lambda j: ((zz * 4 + xx) * 2 + j, rep)
+    if name == "x":
+        return min(4, n_dom // 2), xx, lambda j: ((zz * 4 + j) * 2 + core, rep)
+    if name == "y":
+        return n_rep, rep, lambda j: (dom, j)
+    return max(1, n_dom // 8), zz, lambda j: ((j * 4 + xx) * 2 + core, rep)
+
+
+def _sum_rows(parts, dst, rows):
+    step = min(rows, 64)
+
+    def body(i, carry):
+        at = pl.ds(pl.multiple_of(i * step, 8), step)
+        total = parts[0](at)
+        for part in parts[1:]:
+            total = total + part(at)
+        dst[at, :] = total
+        return carry
+
+    lax.fori_loop(0, rows // step, body, 0)
+
+
+def _reduce_kernel(rs, ag, sizes, x_ref, out_ref, *scratch):
+    n_dom, n_rep = sizes
+    dom = lax.axis_index("dom")
+    rep = lax.axis_index("rep")
+    mesh_id = pl.DeviceIdType.MESH
+    rs_info = [_stage(n, dom, rep, n_dom, n_rep) for n in rs]
+    ag_info = [_stage(n, dom, rep, n_dom, n_rep) for n in ag]
+    nr = len(rs)
+    recv_bufs = scratch[:nr]
+    acc_bufs = scratch[nr : 2 * nr]
+    full = scratch[2 * nr]
+    rs_send, rs_recv, ag_send, ag_recv = scratch[2 * nr + 1 : 2 * nr + 5]
+
+    barrier = pltpu.get_barrier_semaphore()
+    greeted = 0
+    seen = set()
+    for name, (g, c, peer) in zip(list(rs) + list(ag), rs_info + ag_info):
+        if name in seen:
+            continue
+        seen.add(name)
+        for k in range(1, g):
+            pl.semaphore_signal(barrier, 1, device_id=peer((c + k) % g), device_id_type=mesh_id)
+            greeted += 1
+    pl.semaphore_wait(barrier, greeted)
+
+    sends = []
+    src = x_ref
+    length = x_ref.shape[0]
+    base = 0
+    si = 0
+    for s, (g, c, peer) in enumerate(rs_info):
+        piece = length // g
+        for k in range(1, g):
+            j = (c + k) % g
+            cp = pltpu.make_async_remote_copy(
+                src_ref=src.at[pl.ds(pl.multiple_of(j * piece, 8), piece)],
+                dst_ref=recv_bufs[s].at[g - k - 1],
+                send_sem=rs_send.at[si + k - 1],
+                recv_sem=rs_recv.at[si + g - k - 1],
+                device_id=peer(j),
+                device_id_type=mesh_id,
+            )
+            cp.start()
+            sends.append(cp)
+        for k in range(1, g):
+            j = (c + k) % g
+            pltpu.make_async_remote_copy(
+                src_ref=src.at[pl.ds(0, piece)],
+                dst_ref=recv_bufs[s].at[k - 1],
+                send_sem=rs_send.at[si + k - 1],
+                recv_sem=rs_recv.at[si + k - 1],
+                device_id=peer(j),
+                device_id_type=mesh_id,
+            ).wait_recv()
+        own = pl.multiple_of(c * piece, 8)
+        parts = [lambda at, src=src, own=own: src[pl.ds(own + at.start, at.size), :]]
+        for k in range(1, g):
+            parts.append(lambda at, b=recv_bufs[s], k=k: b[k - 1, at, :])
+        _sum_rows(parts, acc_bufs[s], piece)
+        src = acc_bufs[s]
+        base = base + c * piece
+        length = piece
+        si += g - 1
+
+    if not ag_info:
+        out_ref[...] = src[...]
+    else:
+        full[pl.ds(pl.multiple_of(base, 8), length), :] = src[...]
+        ai = 0
+        for g, c, peer in ag_info:
+            mine = pl.ds(pl.multiple_of(base, 8), length)
+            for k in range(1, g):
+                j = (c + k) % g
+                cp = pltpu.make_async_remote_copy(
+                    src_ref=full.at[mine],
+                    dst_ref=full.at[mine],
+                    send_sem=ag_send.at[ai + k - 1],
+                    recv_sem=ag_recv.at[ai + g - k - 1],
+                    device_id=peer(j),
+                    device_id_type=mesh_id,
+                )
+                cp.start()
+                sends.append(cp)
+            start = base - c * length
+            for k in range(1, g):
+                j = (c + k) % g
+                theirs = pl.ds(pl.multiple_of(start + j * length, 8), length)
+                pltpu.make_async_remote_copy(
+                    src_ref=full.at[theirs],
+                    dst_ref=full.at[theirs],
+                    send_sem=ag_send.at[ai + k - 1],
+                    recv_sem=ag_recv.at[ai + k - 1],
+                    device_id=peer(j),
+                    device_id_type=mesh_id,
+                ).wait_recv()
+            base = start
+            length = length * g
+            ai += g - 1
+        out_ref[...] = full[...]
+    for cp in sends:
+        cp.wait_send()
+
+
+def tree_reduce(x, rs, ag, collective_id):
+    n_dom = lax.axis_size("dom")
+    n_rep = lax.axis_size("rep")
+    rows, columns = x.shape
+    shapes = []
+    length = rows
+    rs_sizes = []
+    for name in rs:
+        g = _stage(name, 0, 0, n_dom, n_rep)[0]
+        rs_sizes.append(g)
+    accs = []
+    for g in rs_sizes:
+        piece = length // g
+        shapes.append(pltpu.VMEM((max(g - 1, 1), piece, columns), jnp.float32))
+        accs.append(pltpu.VMEM((piece, columns), jnp.float32))
+        length = piece
+    n_ag = sum(_stage(name, 0, 0, n_dom, n_rep)[0] - 1 for name in ag)
+    out_rows = rows if ag else length
+    scratch = shapes + accs + [
+        pltpu.VMEM((rows if ag else 8, columns), jnp.float32),
+        pltpu.SemaphoreType.DMA((max(1, sum(g - 1 for g in rs_sizes)),)),
+        pltpu.SemaphoreType.DMA((max(1, sum(g - 1 for g in rs_sizes)),)),
+        pltpu.SemaphoreType.DMA((max(1, n_ag),)),
+        pltpu.SemaphoreType.DMA((max(1, n_ag),)),
+    ]
+    return pl.pallas_call(
+        functools.partial(_reduce_kernel, tuple(rs), tuple(ag), (n_dom, n_rep)),
+        out_shape=jax.ShapeDtypeStruct((out_rows, columns), jnp.float32),
+        in_specs=[pl.BlockSpec(memory_space=pltpu.VMEM)],
+        out_specs=pl.BlockSpec(memory_space=pltpu.VMEM),
+        scratch_shapes=scratch,
+        compiler_params=pltpu.CompilerParams(
+            collective_id=collective_id, has_side_effects=True, vmem_limit_bytes=60 * 1024 * 1024
+        ),
+        cost_estimate=pl.CostEstimate(
+            flops=rows * columns * 2, transcendentals=0, bytes_accessed=rows * columns * 16
+        ),
+    )(x)
 
 
 def local(entities, relations, head_local, rel_ids, tail_part, tail_local, neg_local):
@@ -70,9 +241,6 @@
         factor * ((prob_pos - 1.0)[:, None] * tail_embed.astype(jnp.float32) + mixed)
     ).astype(jnp.bfloat16)
     tail_grad = factor * (prob_pos - 1.0)[:, None] * queries.astype(jnp.float32)
-    neg_grad = factor * lax.dot_general(
-        prob_neg, queries, (((0,), (0,)), ((), ())), preferred_element_type=jnp.float32
-    )
     head_grad = jnp.zeros((edge_count, columns), jnp.float32)
     rel_terms = []
     for relation in range(relation_count):
@@ -92,7 +260,15 @@
                 preferred_element_type=jnp.float32,
             )
         )
-    relation_grad = lax.psum(jnp.stack(rel_terms), ("dom", "rep"))
+    rel_stack, prob_neg_late, queries_late = lax.optimization_barrier(
+        (jnp.stack(rel_terms), prob_neg, queries)
+    )
+    relation_grad = tree_reduce(
+        rel_stack.reshape(-1, columns), ("core", "x", "y", "z"), ("z", "y", "x", "core"), 0
+    ).reshape(rel_stack.shape)
+    neg_grad = factor * lax.dot_general(
+        prob_neg_late, queries_late, (((0,), (0,)), ((), ())), preferred_element_type=jnp.float32
+    )
     grad_send = jnp.where(filled[:, None], jnp.take(tail_grad, source, axis=0), 0.0)
     grad_recv = lax.all_to_all(
         grad_send.reshape(part_count, capacity, columns),
@@ -101,7 +277,10 @@
         concat_axis=0,
         tiled=True,
     )
-    owned = lax.psum_scatter(neg_grad, "dom", scatter_dimension=0, tiled=True)
+    neg_parts = lax.all_to_all(
+        neg_grad.reshape(part_count, -1, columns), "dom", split_axis=0, concat_axis=0, tiled=True
+    )
+    owned = jnp.sum(neg_parts, axis=0)
     target_ids = jnp.concatenate([head_local, recv_ids.reshape(-1), neg_local])
     target_rows = jnp.concatenate(
         [head_grad, grad_recv.reshape(slot_count, columns), owned], axis=0

time: 597 us -> 397 us (0.66)
  waiting for transfers between devices: 464 us -> 162 us
  Pallas kernels: 0 us -> 99 us
  starting transfers between devices: 12 us -> 19.5 us
    psum x1 -> x0, waiting for transfers between devices: 259 us -> none  [local(): relation_grad = lax.psum(jnp.stack(rel_terms), ('dom', 'rep'))]
    pallas_call x0 -> x1, Pallas kernels: none -> 99 us  [tree_reduce(): pl.pallas_call(functools.partial(_reduce_kernel, tuple(rs), tuple(ag), (n...]
    all_to_all x0 -> x1, waiting for transfers between devices: none -> 88.6 us  [local(): lax.all_to_all(neg_grad.reshape(part_count, -1, columns), 'dom', split_ax...]
    reduce_scatter x1 -> x0, waiting for transfers between devices: 71.1 us -> none  [local(): owned = lax.psum_scatter(neg_grad, 'dom', scatter_dimension=0, tiled=True)]
    psum x1, waiting for transfers between devices: 67 us -> 0.02 us  [local(): entity_grad = lax.psum(local_grad, 'rep')]
    all_to_all x0 -> x1, starting transfers between devices: none -> 7.55 us  [local(): lax.all_to_all(neg_grad.reshape(part_count, -1, columns), 'dom', split_ax...]
  transfers between devices with their start and end apart: 6 -> 5, of which waited for: 6 -> 4; matrix products, arithmetic and copies ran while one was open for 11% -> 10% of each run, Pallas kernels for 0% -> 25%
where the time goes in v1:
time: 397 us; the launch traced here: 396 us
  waiting for transfers between devices  162 us (41%)
  Pallas kernels  99 us (25%)
  matrix products  30.1 us (8%)
  local copies, waits for them, and re-layouts  28.2 us (7%)
  blocking collectives  22.2 us (6%)
  other arithmetic  20.4 us (5%)
  starting transfers between devices  19.5 us (5%)
  between operations  14.5 us (4%)
    pallas_call x1, Pallas kernels, tree_reduce(): pl.pallas_call(functools.partial(_reduce_kernel, tuple(rs), tuple(ag), (n...  99 us
    all_to_all x1, waiting for transfers between devices, local(): lax.all_to_all(neg_grad.reshape(part_count, -1, columns), 'dom', split_ax...  88.6 us
    all_to_all x1, waiting for transfers between devices, local(): lax.all_to_all(grad_send.reshape(part_count, capacity, columns), 'dom', s...  41.5 us
    all_to_all x1, waiting for transfers between devices, local(): lax.all_to_all(looked_up, 'dom', split_axis=0, concat_axis=0, tiled=True)  26.3 us
    all_to_all x1, blocking collectives, local(): lax.all_to_all(send_ids, 'dom', split_axis=0, concat_axis=0, tiled=True)  22.2 us
    dot_general x2, matrix products, add_block(): jnp.dot(hot, target_rows, precision=lax.Precision.HIGHEST, preferred_elem...  12.3 us
  transfers between devices with their start and end apart: 5, of which 4 were waited for; matrix products, arithmetic and copies ran while one was open for 10% of the time, Pallas kernels for 25%

profile of v1, /device:TPU:1, one launch (start us, length us, event | category | flops | bytes accessed | tf_op | source)
XLA Modules:
  0.0 396.2 jit_solution(18161933904055006694)
XLA Ops:
  7.2 0.7 compare_select_fusion.7
  8.0 0.7 compare_and_fusion.4
  8.7 0.6 gather_fusion.2
  9.3 0.7 broadcast_select_fusion.23
  10.0 0.7 fusion.56
  10.7 1.2 reduce-window.6
  11.9 0.2 slice_reduce_fusion
  12.2 0.8 fusion.55
  13.0 0.7 compare_and_fusion.2
  13.7 0.7 select_reduce_fusion
  14.4 0.1 gt.32
  14.6 6.9 %gather_fusion = s32[1024]{0:T(1024)S(1)} fusion(s32[512]{0:T(512)S(1)} %copy-done.2, s32[1024]{0:T(1024)S(1)} %broadcast_clamp_fusion.1), kind=kCustom, calls=%fused_computation.2 | custom fusion | bytes 12288 | tf_op jit(solution)/shard_map/jit(_take)/gather | solution.py:212
  21.5 22.2 %all_to_all.21 = s32[64,1,16]{2,1,0:T(1,128)S(1)} all-to-all(s32[64,1,16]{2,1,0:T(1,128)S(1)} %bitcast.97), channel_id=1, replica_groups=mesh['dom'=64,'rep'=4] {'dom'}, dimensions={0} | all-to-all | bytes 8192 | tf_op jit(solution)/shard_map/all_to_all | solution.py:215
  43.8 4.0 %gather_fusion.1 = bf16[1024,512]{1,0:T(8,128)(2,1)S(1)} fusion(bf16[1024,512]{1,0:T(8,128)(2,1)S(1)} %copy-done, s32[1024]{0:T(1024)S(1)} %broadcast_clamp_fusion), kind=kCustom, calls=%fused_computation.3 | custom fusion | bytes 2101248 | tf_op jit(solution)/shard_map/jit(_take)/gather | solution.py:216
  47.8 1.2 broadcast_select_fusion
  49.0 4.8 %all-to-all-start.1 = ((bf16[64,16,512]{2,1,0:T(8,128)(2,1)}), bf16[64,16,512]{2,1,0:T(8,128)(2,1)S(1)}, u32[]{:S(2)}, u32[]{:S(2)}) async-start(bf16[64,16,512]{2,1,0:T(8,128)(2,1)} %broadcast_select_fusion), calls=%async_computation.1 | async-start | bytes 2097152 | tf_op jit(solution)/shard_map/all_to_all | solution.py:219
  53.8 2.0 gather_fusion.4
  55.8 0.2 copy.27
  56.1 1.7 fusion.23
  57.8 0.5 convolution_add_fusion.5
  58.2 0.5 convolution_add_fusion.4
  58.7 26.3 %all-to-all-done.1 = bf16[64,16,512]{2,1,0:T(8,128)(2,1)S(1)} async-done(((bf16[64,16,512]{2,1,0:T(8,128)(2,1)}), bf16[64,16,512]{2,1,0:T(8,128)(2,1)S(1)}, u32[]{:S(2)}, u32[]{:S(2)}) %all-to-all-start.1) | async-done | bytes 1048608 | tf_op jit(solution)/shard_map/all_to_all | solution.py:219
  85.0 2.0 gather_fusion.5
  87.0 0.2 copy.28
  87.2 1.6 fusion.14
  88.8 5.7 %all-gather.2.cloned.1.call-done = bf16[2048,512]{1,0:T(8,128)(2,1)} async-done(((bf16[32,512]{1,0:T(8,128)(2,1)}), bf16[2048,512]{1,0:T(8,128)(2,1)}) %all-gather.2.cloned.1.call-update) | async-done | bytes 2097168 | tf_op jit(solution)/shard_map/all_gather | solution.py:222
  94.5 3.0 multiply_reduce_fusion
  97.5 0.8 fusion.10
  98.3 0.6 broadcast_multiply_fusion
  98.9 0.8 divide_convert_fusion
  99.8 0.7 copy-done.9
  100.5 1.3 fusion.12
  101.9 0.5 convolution_bitcast_fusion
  102.3 0.5 convolution_bitcast_fusion.1
  102.8 0.5 convolution_bitcast_fusion.2
  103.3 0.5 convolution_bitcast_fusion.3
  103.8 2.4 pad_maximum_fusion
  106.2 3.3 convolution_multiply_fusion
  109.5 7.6 %all-to-all-start.3 = ((f32[64,32,512]{2,1,0:T(8,128)}), f32[64,32,512]{2,1,0:T(8,128)}, u32[]{:S(2)}, u32[]{:S(2)}) async-start(f32[64,32,512]{2,1,0:T(8,128)} %bitcast.88), calls=%async_computation.3 | async-start | bytes 8388608 | tf_op jit(solution)/shard_map/all_to_all | solution.py:280
  117.2 0.1 convert_multiply_fusion.2
  117.4 0.3 copy.30
  117.7 3.5 gather_fusion.3
  121.2 1.6 select_select_fusion
  122.9 88.6 %all-to-all-done.3 = f32[64,32,512]{2,1,0:T(8,128)} async-done(((f32[64,32,512]{2,1,0:T(8,128)}), f32[64,32,512]{2,1,0:T(8,128)}, u32[]{:S(2)}, u32[]{:S(2)}) %all-to-all-start.3) | async-done | bytes 4194336 | tf_op jit(solution)/shard_map/all_to_all | solution.py:280
  211.5 7.1 %all-to-all-start.2 = ((f32[64,16,512]{2,1,0:T(8,128)}), f32[64,16,512]{2,1,0:T(8,128)S(1)}, u32[]{:S(2)}, u32[]{:S(2)}) async-start(f32[64,16,512]{2,1,0:T(8,128)} %select_select_fusion), calls=%async_computation.2 | async-start | bytes 4194304 | tf_op jit(solution)/shard_map/all_to_all | solution.py:273
  218.7 0.5 broadcast.287
  219.2 0.7 reduce.7
  220.0 1.7 fusion.21
  221.8 0.5 convolution_add_fusion.2
  222.3 0.5 convolution_add_fusion.1
  222.8 1.5 convolution_add_fusion
  224.2 2.6 reduce_sum.68
  226.8 41.5 %all-to-all-done.2 = f32[64,16,512]{2,1,0:T(8,128)S(1)} async-done(((f32[64,16,512]{2,1,0:T(8,128)}), f32[64,16,512]{2,1,0:T(8,128)S(1)}, u32[]{:S(2)}, u32[]{:S(2)}) %all-to-all-start.2) | async-done | bytes 2097184 | tf_op jit(solution)/shard_map/all_to_all | solution.py:273
  268.3 2.0 pad_maximum_fusion.1
  270.3 14.7 %while.10 = (s32[]{:T(128)}, f32[2,512,512]{2,1,0:T(8,128)}, s32[1568]{0:T(1024)S(1)}, s32[2]{0:T(128)S(1)}, f32[1568,512]{1,0:T(8,128)}, /*index=5*/s32[]{:T(128)}) while((s32[]{:T(128)}, f32[2,512,512]{2,1,0:T(8,128)}, s32[1568]{0:T(1024)S(1)}, s32[2]{0:T(128)S(1)}, f32[1568,512]{1,0:T(8,128)}, /*index=5*/s32[]{:T(128)}) %tuple.36), condition=%wide.region_10.12_spmd, body=%wide.region_9.11_spmd.sunk | while | flops 4933304832 | bytes 4270305 | solution.py:299
  270.3 0.6 dynamic_slice.5
  270.9 0.6 iota_add_fusion.2
  271.5 6.1 %fusion.94 = f32[2,512,512]{2,1,0:T(8,128)} fusion(f32[2,512,512]{2,1,0:T(8,128)} %get-tuple-element.103, s32[]{:T(128)S(6)} %copy.37, f32[1568,512]{1,0:T(8,128)} %get-tuple-element.112, s32[1568]{0:T(1024)S(1)} %get-tuple-element.110, s32[512]{0:T(512)S(1)} %iota_add_fusion.2), kind=kOutput, calls=%fused_computation.11.clone.1 | convolution fusion | flops 4933304320 | bytes 4268164 | tf_op jit(solution)/shard_map/while/body/eval_jaxpr/dot_general | solution.py:295
  277.6 0.6 dynamic_slice.5
  278.2 0.6 iota_add_fusion.2
  278.8 6.1 %fusion.94 = f32[2,512,512]{2,1,0:T(8,128)} fusion(f32[2,512,512]{2,1,0:T(8,128)} %get-tuple-element.103, s32[]{:T(128)S(6)} %copy.37, f32[1568,512]{1,0:T(8,128)} %get-tuple-element.112, s32[1568]{0:T(1024)S(1)} %get-tuple-element.110, s32[512]{0:T(512)S(1)} %iota_add_fusion.2), kind=kOutput, calls=%fused_computation.11.clone.1 | convolution fusion | flops 4933304320 | bytes 4268164 | tf_op jit(solution)/shard_map/while/body/eval_jaxpr/dot_general | solution.py:295
  285.0 99.0 %shard_map.94 = f32[2048,512]{1,0:T(8,128)} custom-call(f32[2048,512]{1,0:T(8,128)} %bitcast.89), custom_call_target="tpu_custom_call" | custom-call | flops 2097152 | bytes 16777216 | tf_op jit(solution)/shard_map/pallas_call | solution.py:167
  384.1 3.2 copy.45
  387.3 2.0 copy.46
  (56 shorter events, 0.9 us)
Async XLA Ops:
  7.2 1.5 copy-start
  7.2 7.4 %copy-start.2 = (s32[512]{0:T(512)S(1)}, s32[512]{0:T(512)}, u32[]{:S(2)}) copy-start(s32[512]{0:T(512)} %param.16) | copy-start | bytes 6148
  7.2 87.3 %all-gather.2.cloned.1.call-start = ((), (), s32[]{:S(2)}) async-start(), calls=%async_computation.4 | async-start | bytes 2129920 | tf_op jit(solution)/shard_map/all_gather | solution.py:222
  47.8 6.0 %copy-start.10 = (s32[512]{0:T(512)S(1)}, s32[512]{0:T(512)}, u32[]{:S(2)}) copy-start(s32[512]{0:T(512)} %param.13) | copy-start | bytes 6148
  49.0 36.0 %all-to-all-start.1 = ((bf16[64,16,512]{2,1,0:T(8,128)(2,1)}), bf16[64,16,512]{2,1,0:T(8,128)(2,1)S(1)}, u32[]{:S(2)}, u32[]{:S(2)}) async-start(bf16[64,16,512]{2,1,0:T(8,128)(2,1)} %broadcast_select_fusion), calls=%async_computation.1 | async-start | bytes 2097152 | tf_op jit(solution)/shard_map/all_to_all | solution.py:219
  53.8 2.2 copy-start.11
  56.0 1.8 copy-start.7
  98.9 1.6 copy-start.9
  101.9 1.4 copy-start.4
  109.5 102.0 %all-to-all-start.3 = ((f32[64,32,512]{2,1,0:T(8,128)}), f32[64,32,512]{2,1,0:T(8,128)}, u32[]{:S(2)}, u32[]{:S(2)}) async-start(f32[64,32,512]{2,1,0:T(8,128)} %bitcast.88), calls=%async_computation.3 | async-start | bytes 8388608 | tf_op jit(solution)/shard_map/all_to_all | solution.py:280
  122.8 97.2 %copy-start.12 = (s32[32]{0:T(128)S(1)}, s32[32]{0:T(128)}, u32[]{:S(2)}) copy-start(s32[32]{0:T(128)} %param.17) | copy-start | bytes 388
  122.9 97.2 %copy-start.5 = (bf16[512,512]{0,1:T(8,128)(2,1)S(1)}, bf16[512,512]{0,1:T(8,128)(2,1)}, u32[]{:S(2)}) copy-start(bf16[512,512]{0,1:T(8,128)(2,1)} %copy-done.4) | copy-start | bytes 1572868
  211.5 56.8 %all-to-all-start.2 = ((f32[64,16,512]{2,1,0:T(8,128)}), f32[64,16,512]{2,1,0:T(8,128)S(1)}, u32[]{:S(2)}, u32[]{:S(2)}) async-start(f32[64,16,512]{2,1,0:T(8,128)} %select_select_fusion), calls=%async_computation.2 | async-start | bytes 4194304 | tf_op jit(solution)/shard_map/all_to_all | solution.py:273
  218.6 165.5 %all-reduce.2.cloned.1.call-start = ((), (), s32[]{:S(2)}) async-start(), calls=%async_computation.5 | async-start | bytes 4194304 | tf_op jit(solution)/shard_map/psum | solution.py:302
  220.0 1.8 copy-start.8
  224.2 44.1 %copy-start.6 = (f32[512,512]{1,0:T(8,128)S(1)}, f32[512,512]{1,0:T(8,128)}, u32[]{:S(2)}) copy-start(f32[512,512]{1,0:T(8,128)} %convolution_add_fusion) | copy-start | bytes 3145732
  384.1 3.2 copy-start.3
  387.3 2.0 copy-start.1
Sparse Core Ops, SparseCore 0:
  11.4 83.1 all-gather.1
  285.1 65.2 all-reduce.1

commit v2 on v1

--- a/solution.py
+++ b/solution.py
@@ -179,6 +179,210 @@
     )(x)
 
 
+def _lane_kernel(lanes, sizes, n_in, *refs):
+    n_dom, n_rep = sizes
+    ins = refs[:n_in]
+    outs = refs[n_in : 2 * n_in]
+    scratch = refs[2 * n_in :]
+    dom = lax.axis_index("dom")
+    rep = lax.axis_index("rep")
+    mesh_id = pl.DeviceIdType.MESH
+    pos = 0
+    lane_bufs = []
+    for _, _, _, rs, _ in lanes:
+        lane_bufs.append((scratch[pos : pos + len(rs)], scratch[pos + len(rs) : pos + 2 * len(rs)]))
+        pos += 2 * len(rs)
+    fulls = scratch[pos : pos + n_in]
+    rs_send, rs_recv, ag_send, ag_recv = scratch[pos + n_in : pos + n_in + 4]
+
+    def info(name):
+        return _stage(name, dom, rep, n_dom, n_rep)
+
+    barrier = pltpu.get_barrier_semaphore()
+    greeted = 0
+    names = []
+    for lane in lanes:
+        for name in lane[3] + lane[4]:
+            if name not in names:
+                names.append(name)
+    for name in names:
+        g, c, peer = info(name)
+        for k in range(1, g):
+            pl.semaphore_signal(barrier, 1, device_id=peer((c + k) % g), device_id_type=mesh_id)
+            greeted += 1
+    pl.semaphore_wait(barrier, greeted)
+
+    sends = []
+    state = [
+        (ins[i], c0, w, ins[i].shape[0], 0) for i, c0, w, _, _ in lanes
+    ]
+    rs_base = []
+    total = 0
+    for lane in lanes:
+        rs_base.append(total)
+        total += sum(info(name)[0] - 1 for name in lane[3])
+    for t in range(max(len(lane[3]) for lane in lanes)):
+        pending = []
+        offsets = [rs_base[li] + sum(info(n)[0] - 1 for n in lane[3][:t]) for li, lane in enumerate(lanes)]
+        for li, lane in enumerate(lanes):
+            if t >= len(lane[3]):
+                continue
+            g, c, peer = info(lane[3][t])
+            ref, c0, w, length, gbase = state[li]
+            piece = length // g
+            si = offsets[li]
+            recv = lane_bufs[li][0][t]
+            for k in range(1, g):
+                j = (c + k) % g
+                cp = pltpu.make_async_remote_copy(
+                    src_ref=ref.at[pl.ds(pl.multiple_of(j * piece, 8), piece), pl.ds(c0, w)],
+                    dst_ref=recv.at[g - k - 1],
+                    send_sem=rs_send.at[si + k - 1],
+                    recv_sem=rs_recv.at[si + g - k - 1],
+                    device_id=peer(j),
+                    device_id_type=mesh_id,
+                )
+                cp.start()
+                sends.append(cp)
+            pending.append(li)
+        for li in pending:
+            lane = lanes[li]
+            g, c, peer = info(lane[3][t])
+            ref, c0, w, length, gbase = state[li]
+            piece = length // g
+            si = offsets[li]
+            recv = lane_bufs[li][0][t]
+            acc = lane_bufs[li][1][t]
+            for k in range(1, g):
+                j = (c + k) % g
+                pltpu.make_async_remote_copy(
+                    src_ref=ref.at[pl.ds(0, piece), pl.ds(c0, w)],
+                    dst_ref=recv.at[k - 1],
+                    send_sem=rs_send.at[si + k - 1],
+                    recv_sem=rs_recv.at[si + k - 1],
+                    device_id=peer(j),
+                    device_id_type=mesh_id,
+                ).wait_recv()
+            own = pl.multiple_of(c * piece, 8)
+            parts = [lambda at, ref=ref, own=own, c0=c0, w=w: ref[pl.ds(own + at.start, at.size), pl.ds(c0, w)]]
+            for k in range(1, g):
+                parts.append(lambda at, b=recv, k=k: b[k - 1, at, :])
+            _sum_rows(parts, acc, piece)
+            state[li] = (acc, 0, w, piece, gbase + c * piece)
+
+    ag_state = []
+    for li, lane in enumerate(lanes):
+        acc, _, w, length, gbase = state[li]
+        i, c0 = lane[0], lane[1]
+        if lane[4]:
+            fulls[i][pl.ds(pl.multiple_of(gbase, 8), length), pl.ds(c0, w)] = acc[...]
+        else:
+            outs[i][...] = acc[...]
+        ag_state.append((length, gbase))
+    ag_base = []
+    total = 0
+    for lane in lanes:
+        ag_base.append(total)
+        total += sum(info(name)[0] - 1 for name in lane[4])
+    for t in range(max(len(lane[4]) for lane in lanes)):
+        pending = []
+        offsets = [ag_base[li] + sum(info(n)[0] - 1 for n in lane[4][:t]) for li, lane in enumerate(lanes)]
+        for li, lane in enumerate(lanes):
+            if t >= len(lane[4]):
+                continue
+            g, c, peer = info(lane[4][t])
+            length, gbase = ag_state[li]
+            full = fulls[lane[0]]
+            cols = pl.ds(lane[1], lane[2])
+            mine = pl.ds(pl.multiple_of(gbase, 8), length)
+            ai = offsets[li]
+            for k in range(1, g):
+                j = (c + k) % g
+                cp = pltpu.make_async_remote_copy(
+                    src_ref=full.at[mine, cols],
+                    dst_ref=full.at[mine, cols],
+                    send_sem=ag_send.at[ai + k - 1],
+                    recv_sem=ag_recv.at[ai + g - k - 1],
+                    device_id=peer(j),
+                    device_id_type=mesh_id,
+                )
+                cp.start()
+                sends.append(cp)
+            pending.append(li)
+        for li in pending:
+            lane = lanes[li]
+            g, c, peer = info(lane[4][t])
+            length, gbase = ag_state[li]
+            full = fulls[lane[0]]
+            cols = pl.ds(lane[1], lane[2])
+            ai = offsets[li]
+            start = gbase - c * length
+            for k in range(1, g):
+                j = (c + k) % g
+                theirs = pl.ds(pl.multiple_of(start + j * length, 8), length)
+                pltpu.make_async_remote_copy(
+                    src_ref=full.at[theirs, cols],
+                    dst_ref=full.at[theirs, cols],
+                    send_sem=ag_send.at[ai + k - 1],
+                    recv_sem=ag_recv.at[ai + k - 1],
+                    device_id=peer(j),
+                    device_id_type=mesh_id,
+                ).wait_recv()
+            ag_state[li] = (length * g, start)
+    gathered = sorted({lane[0] for lane in lanes if lane[4]})
+    for i in gathered:
+        outs[i][...] = fulls[i][...]
+    for cp in sends:
+        cp.wait_send()
+
+
+def lane_reduce(inputs, lanes, collective_id):
+    n_dom = lax.axis_size("dom")
+    n_rep = lax.axis_size("rep")
+    scratch = []
+    recv_shapes, acc_shapes = [], []
+    n_rs = n_ag = 0
+    out_shapes = [None] * len(inputs)
+    for i, c0, w, rs, ag in lanes:
+        length = inputs[i].shape[0]
+        recv, accs = [], []
+        for name in rs:
+            g = _stage(name, 0, 0, n_dom, n_rep)[0]
+            piece = length // g
+            recv.append(pltpu.VMEM((max(g - 1, 1), piece, w), jnp.float32))
+            accs.append(pltpu.VMEM((piece, w), jnp.float32))
+            length = piece
+            n_rs += g - 1
+        n_ag += sum(_stage(name, 0, 0, n_dom, n_rep)[0] - 1 for name in ag)
+        scratch += recv + accs
+        out_shapes[i] = inputs[i].shape if ag else (length, w)
+    for i, x in enumerate(inputs):
+        scratch.append(pltpu.VMEM(x.shape if any(l[0] == i and l[4] for l in lanes) else (8, 128), jnp.float32))
+    scratch += [
+        pltpu.SemaphoreType.DMA((max(1, n_rs),)),
+        pltpu.SemaphoreType.DMA((max(1, n_rs),)),
+        pltpu.SemaphoreType.DMA((max(1, n_ag),)),
+        pltpu.SemaphoreType.DMA((max(1, n_ag),)),
+    ]
+    moved = sum(x.size for x in inputs) * 4
+    return pl.pallas_call(
+        functools.partial(_lane_kernel, tuple(lanes), (n_dom, n_rep), len(inputs)),
+        out_shape=[jax.ShapeDtypeStruct(shape, jnp.float32) for shape in out_shapes],
+        in_specs=[pl.BlockSpec(memory_space=pltpu.VMEM)] * len(inputs),
+        out_specs=[pl.BlockSpec(memory_space=pltpu.VMEM)] * len(inputs),
+        scratch_shapes=scratch,
+        compiler_params=pltpu.CompilerParams(
+            collective_id=collective_id, has_side_effects=True, vmem_limit_bytes=62 * 1024 * 1024
+        ),
+        cost_estimate=pl.CostEstimate(flops=moved, transcendentals=0, bytes_accessed=moved * 4),
+    )(*inputs)
+
+
+def pick_rows(table, ids):
+    hot = (ids[:, None] == jnp.arange(table.shape[0], dtype=ids.dtype)[None, :]).astype(table.dtype)
+    return jnp.dot(hot, table, preferred_element_type=jnp.float32).astype(table.dtype)
+
+
 def local(entities, relations, head_local, rel_ids, tail_part, tail_local, neg_local):
     factor = 1.0 / math.sqrt(D)
     ent_dev = entities.shape[0]
@@ -188,7 +392,7 @@
     capacity = 2 * edge_count // part_count
     slot_count = part_count * capacity
     relation_count = relations.shape[0]
-    head_rows = jnp.take(entities, head_local, axis=0)
+    head_rows = pick_rows(entities, head_local)
     selectors = [(rel_ids == relation)[:, None] for relation in range(relation_count)]
     query_sum = jnp.zeros((edge_count, columns), jnp.float32)
     for relation in range(relation_count):
@@ -213,11 +417,11 @@
         part_count, capacity
     )
     recv_ids = lax.all_to_all(send_ids, "dom", split_axis=0, concat_axis=0, tiled=True)
-    looked_up = jnp.take(entities, recv_ids.reshape(-1), axis=0).reshape(
+    looked_up = pick_rows(entities, recv_ids.reshape(-1)).reshape(
         part_count, capacity, columns
     )
     returned = lax.all_to_all(looked_up, "dom", split_axis=0, concat_axis=0, tiled=True)
-    tail_embed = jnp.take(returned.reshape(slot_count, columns), slot_index, axis=0)
+    tail_embed = pick_rows(returned.reshape(slot_count, columns), slot_index)
     own_negs = jnp.take(entities, neg_local, axis=0)
     negatives = lax.all_gather(own_negs, "dom", axis=0, tiled=True)
     positive = (
@@ -263,25 +467,48 @@
     rel_stack, prob_neg_late, queries_late = lax.optimization_barrier(
         (jnp.stack(rel_terms), prob_neg, queries)
     )
-    relation_grad = tree_reduce(
-        rel_stack.reshape(-1, columns), ("core", "x", "y", "z"), ("z", "y", "x", "core"), 0
-    ).reshape(rel_stack.shape)
     neg_grad = factor * lax.dot_general(
         prob_neg_late, queries_late, (((0,), (0,)), ((), ())), preferred_element_type=jnp.float32
     )
-    grad_send = jnp.where(filled[:, None], jnp.take(tail_grad, source, axis=0), 0.0)
-    grad_recv = lax.all_to_all(
-        grad_send.reshape(part_count, capacity, columns),
+    scale = factor * (prob_pos - 1.0)
+    scale_hi = lax.reduce_precision(scale, exponent_bits=8, mantissa_bits=7)
+    scale_rest = scale - scale_hi
+    scale_mid = lax.reduce_precision(scale_rest, exponent_bits=8, mantissa_bits=7)
+    scale_lo = scale_rest - scale_mid
+    pack = jnp.concatenate(
+        [
+            queries,
+            jnp.stack([scale_hi, scale_mid, scale_lo], axis=1).astype(jnp.bfloat16),
+            jnp.zeros((edge_count, 125), jnp.bfloat16),
+        ],
+        axis=1,
+    )
+    pack_send = jnp.dot(
+        slot_match.astype(jnp.bfloat16), pack, preferred_element_type=jnp.float32
+    ).astype(jnp.bfloat16)
+    pack_recv = lax.all_to_all(
+        pack_send.reshape(part_count, capacity, pack.shape[1]),
         "dom",
         split_axis=0,
         concat_axis=0,
         tiled=True,
-    )
-    neg_parts = lax.all_to_all(
-        neg_grad.reshape(part_count, -1, columns), "dom", split_axis=0, concat_axis=0, tiled=True
-    )
-    owned = jnp.sum(neg_parts, axis=0)
-    target_ids = jnp.concatenate([head_local, recv_ids.reshape(-1), neg_local])
+    ).reshape(slot_count, pack.shape[1])
+    recv_scale = (
+        pack_recv[:, columns].astype(jnp.float32) + pack_recv[:, columns + 1].astype(jnp.float32)
+    ) + pack_recv[:, columns + 2].astype(jnp.float32)
+    grad_recv = recv_scale[:, None] * pack_recv[:, :columns].astype(jnp.float32)
+    rep_count = lax.axis_size("rep")
+    neg_order = neg_grad.reshape(part_count // 8, 4, 2, rep_count, -1, columns)
+    neg_order = neg_order.transpose(2, 3, 1, 0, 4, 5).reshape(-1, columns)
+    orders = (("core", "x", "y", "z"), ("core", "y", "x", "z"))
+    width = columns // len(orders)
+    lanes = [(0, width * i, width, order, order[::-1]) for i, order in enumerate(orders)]
+    lanes.append((1, 0, columns, ("core", "y", "x", "z"), ()))
+    relation_flat, owned = lane_reduce([rel_stack.reshape(-1, columns), neg_order], lanes, 0)
+    relation_grad = relation_flat.reshape(rel_stack.shape)
+    neg_rows = owned.shape[0]
+    neg_ids = lax.dynamic_slice_in_dim(neg_local, lax.axis_index("rep") * neg_rows, neg_rows)
+    target_ids = jnp.concatenate([head_local, recv_ids.reshape(-1), neg_ids])
     target_rows = jnp.concatenate(
         [head_grad, grad_recv.reshape(slot_count, columns), owned], axis=0
     )
@@ -299,7 +526,7 @@
     local_grad = lax.map(add_block, jnp.arange(block_count, dtype=jnp.int32) * block_rows).reshape(
         ent_dev, columns
     )
-    entity_grad = lax.psum(local_grad, "rep")
+    entity_grad = tree_reduce(local_grad, ("y",), ("y",), 2)
     return (entity_grad, relation_grad, edge_loss)
 
 

time: 397 us -> 318 us (0.80)
  waiting for transfers between devices: 162 us -> 45.2 us
  Pallas kernels: 99 us -> 159 us
  blocking collectives: 22.2 us -> 0 us
  local copies, waits for them, and re-layouts: 28.2 us -> 19.5 us
  starting transfers between devices: 19.5 us -> 25.4 us
    all_to_all x2, waiting for transfers between devices: 130 us -> 9.27 us  [the longest x1 9.27 us: local(): lax.all_to_all(send_ids, 'dom', split_axis=0, concat_axis=0, tiled=True)]
    pallas_call x0 -> x1, Pallas kernels: none -> 105 us  [lane_reduce(): pl.pallas_call(functools.partial(_lane_kernel, tuple(lanes), (n_dom, n_re...]
    pallas_call x1, Pallas kernels: 99 us -> 53.8 us  [tree_reduce(): pl.pallas_call(functools.partial(_reduce_kernel, tuple(rs), tuple(ag), (n...]
    all_to_all x1 -> x0, blocking collectives: 22.2 us -> none  [local(): lax.all_to_all(send_ids, 'dom', split_axis=0, concat_axis=0, tiled=True)]
    gather x6 -> x0, local copies, waits for them, and re-layouts: 11.8 us -> none  [the longest x1 3.97 us: local(): jnp.take(entities, recv_ids.reshape(-1), axis=0)]
    dot_general x0 -> x4, matrix products: none -> 6.64 us  [the longest x3 4.57 us: pick_rows(): jnp.dot(hot, table, preferred_element_type=jnp.float32).astype(table.dtype)]
    all_to_all x2, starting transfers between devices: 14.7 us -> 20.5 us  [the longest x1 13 us: local(): lax.all_to_all(send_ids, 'dom', split_axis=0, concat_axis=0, tiled=True)]
  transfers between devices with their start and end apart: 5 -> 4, of which waited for: 4 -> 3; matrix products, arithmetic and copies ran while one was open for 10% -> 11% of each run, Pallas kernels for 25% -> 33%
where the time goes in v2:
time: 318 us
  Pallas kernels  159 us (50%)
  waiting for transfers between devices  45.2 us (14%)
  matrix products  34 us (11%)
  starting transfers between devices  25.4 us (8%)
  other arithmetic  19.9 us (6%)
  local copies, waits for them, and re-layouts  19.5 us (6%)
  between operations  14.4 us (5%)
    pallas_call x1, Pallas kernels, lane_reduce(): pl.pallas_call(functools.partial(_lane_kernel, tuple(lanes), (n_dom, n_re...  105 us
    pallas_call x1, Pallas kernels, tree_reduce(): pl.pallas_call(functools.partial(_reduce_kernel, tuple(rs), tuple(ag), (n...  53.8 us
    all_to_all x1, waiting for transfers between devices, local(): lax.all_to_all(looked_up, 'dom', split_axis=0, concat_axis=0, tiled=True)  27.3 us
    all_to_all x1, starting transfers between devices, local(): lax.all_to_all(send_ids, 'dom', split_axis=0, concat_axis=0, tiled=True)  13 us
    dot_general x2, matrix products, add_block(): jnp.dot(hot, target_rows, precision=lax.Precision.HIGHEST, preferred_elem...  12.2 us
    all_to_all x1, waiting for transfers between devices, local(): lax.all_to_all(send_ids, 'dom', split_axis=0, concat_axis=0, tiled=True)  9.27 us
    all_gather x1, waiting for transfers between devices, local(): negatives = lax.all_gather(own_negs, 'dom', axis=0, tiled=True)  8.66 us
    all_to_all x1, starting transfers between devices, local(): lax.all_to_all(pack_send.reshape(part_count, capacity, pack.shape[1]), 'd...  7.49 us
  transfers between devices with their start and end apart: 4, of which 3 were waited for; matrix products, arithmetic and copies ran while one was open for 11% of the time, Pallas kernels for 33%

profile of v2, /device:TPU:1, one launch (start us, length us, event | category | flops | bytes accessed | tf_op | source)
XLA Modules:
  0.0 317.7 jit_solution(14120704092366766615)
XLA Ops:
  7.2 0.7 compare_select_fusion.2
  8.0 0.7 compare_and_fusion
  8.7 0.6 gather_fusion.1
  9.3 0.7 broadcast_select_fusion.12
  10.0 0.7 fusion.58
  10.7 1.2 reduce-window.6
  11.9 0.2 slice_reduce_fusion
  12.2 0.8 fusion.57
  13.0 0.7 multiply_add_fusion.1
  13.7 0.7 select_reduce_fusion
  14.4 6.9 %gather_fusion = s32[1024]{0:T(1024)S(1)} fusion(s32[512]{0:T(512)S(1)} %copy-done.1, s32[1024]{0:T(1024)S(1)} %broadcast_clamp_fusion), kind=kCustom, calls=%fused_computation | custom fusion | bytes 12288 | tf_op jit(solution)/shard_map/jit(_take)/gather | solution.py:416
  21.4 0.1 gt.23
  21.5 0.6 select_select_fusion
  22.1 13.0 %all-to-all-start = ((s32[64,1,16]{2,1,0:T(1,128)}), s32[64,1,16]{2,1,0:T(1,128)S(1)}, u32[]{:S(2)}, u32[]{:S(2)}) async-start(s32[64,1,16]{2,1,0:T(1,128)} %bitcast.7), calls=%async_computation | async-start | bytes 65536 | tf_op jit(solution)/shard_map/all_to_all | solution.py:419
  35.2 9.3 %all-to-all-done = s32[64,1,16]{2,1,0:T(1,128)S(1)} async-done(((s32[64,1,16]{2,1,0:T(1,128)}), s32[64,1,16]{2,1,0:T(1,128)S(1)}, u32[]{:S(2)}, u32[]{:S(2)}) %all-to-all-start) | async-done | bytes 4128 | tf_op jit(solution)/shard_map/all_to_all | solution.py:419
  44.5 0.5 broadcast.265
  45.0 0.7 reduce.7
  45.8 2.3 fusion.15
  48.1 4.9 %all-to-all-start.1 = ((bf16[64,16,512]{2,1,0:T(8,128)(2,1)}), bf16[64,16,512]{2,1,0:T(8,128)(2,1)S(1)}, u32[]{:S(2)}, u32[]{:S(2)}) async-start(bf16[64,16,512]{2,1,0:T(8,128)(2,1)} %bitcast.14), calls=%async_computation.1 | async-start | bytes 2097152 | tf_op jit(solution)/shard_map/all_to_all | solution.py:423
  53.1 0.8 fusion.19
  53.8 0.8 copy-done.3
  54.6 0.5 fusion.33
  55.1 0.5 convolution_add_fusion.5
  55.6 0.5 convolution_add_fusion.4
  56.1 0.5 fusion.20
  56.6 27.3 %all-to-all-done.1 = bf16[64,16,512]{2,1,0:T(8,128)(2,1)S(1)} async-done(((bf16[64,16,512]{2,1,0:T(8,128)(2,1)}), bf16[64,16,512]{2,1,0:T(8,128)(2,1)S(1)}, u32[]{:S(2)}, u32[]{:S(2)}) %all-to-all-start.1) | async-done | bytes 1048608 | tf_op jit(solution)/shard_map/all_to_all | solution.py:423
  83.9 1.5 fusion.21
  85.4 8.7 %all-gather.2.cloned.1.call-done = bf16[2048,512]{1,0:T(8,128)(2,1)} async-done(((bf16[32,512]{1,0:T(8,128)(2,1)}), bf16[2048,512]{1,0:T(8,128)(2,1)}) %all-gather.2.cloned.1.call-update) | async-done | bytes 2097168 | tf_op jit(solution)/shard_map/all_gather | solution.py:426
  94.1 3.0 multiply_reduce_fusion
  97.0 0.8 fusion.11
  97.9 0.6 add_subtract_fusion
  98.5 2.1 divide_convert_fusion
  100.7 0.2 copy.58
  100.8 0.2 copy.59
  101.0 0.2 copy.60
  101.3 0.4 concatenate.11
  101.7 2.1 convolution_convert_fusion
  103.8 7.5 %all-to-all-start.2 = ((bf16[64,16,640]{2,1,0:T(8,128)(2,1)}), bf16[64,16,640]{2,1,0:T(8,128)(2,1)}, u32[]{:S(2)}, u32[]{:S(2)}) async-start(bf16[64,16,640]{2,1,0:T(8,128)(2,1)} %bitcast.19), calls=%async_computation.2 | async-start | bytes 2621440 | tf_op jit(solution)/shard_map/all_to_all | solution.py:489
  111.3 3.6 %fusion.17 = bf16[512,512]{1,0:T(8,128)(2,1)S(1)} fusion(bf16[512,2048]{1,0:T(8,128)(2,1)} %divide_convert_fusion, bf16[2048,512]{1,0:T(8,128)(2,1)} %all-gather.2.cloned.1.call-done, bf16[512,512]{1,0:T(8,128)(2,1)} %get-tuple-element.68, f32[512]{0:T(512)S(1)} %get-tuple-element.56), kind=kOutput, calls=%fused_computation.44 | convolution fusion | flops 1075052544 | bytes 5244928 | tf_op jit(solution)/shard_map/dot_general | solution.py:443
  114.8 0.6 convolution_bitcast_fusion.1
  115.4 0.6 convolution_bitcast_fusion.2
  115.9 0.6 convolution_bitcast_fusion.3
  116.5 0.6 convolution_bitcast_fusion
  117.1 2.5 pad_maximum_fusion
  119.5 1.3 convolution_multiply_fusion
  120.8 2.6 copy.61
  123.4 105.3 %shard_map.94 = (f32[2048,512]{1,0:T(8,128)}, f32[8,512]{1,0:T(8,128)}) custom-call(f32[2048,512]{1,0:T(8,128)} %bitcast.95, f32[2048,512]{1,0:T(8,128)} %bitcast.96), custom_call_target="tpu_custom_call" | custom-call | flops 8388608 | bytes 33554432 | tf_op jit(solution)/shard_map/pallas_call | solution.py:368
  228.8 1.7 fusion.31
  230.5 0.5 convolution_add_fusion.2
  231.0 0.5 convolution_add_fusion.1
  231.5 0.5 convolution_add_fusion
  232.0 1.6 add_reduce_fusion
  233.6 1.4 convert_multiply_fusion
  235.0 2.1 pad_maximum_fusion.1
  237.1 14.7 %while.10 = (s32[]{:T(128)}, f32[2,512,512]{2,1,0:T(8,128)}, s32[1544]{0:T(1024)S(1)}, s32[2]{0:T(128)S(1)}, f32[1544,512]{1,0:T(8,128)}, /*index=5*/s32[]{:T(128)}) while((s32[]{:T(128)}, f32[2,512,512]{2,1,0:T(8,128)}, s32[1544]{0:T(1024)S(1)}, s32[2]{0:T(128)S(1)}, f32[1544,512]{1,0:T(8,128)}, /*index=5*/s32[]{:T(128)}) %tuple.35), condition=%wide.region_9.10_spmd, body=%wide.region_8.9_spmd.sunk | while | flops 4857795072 | bytes 4221557 | solution.py:526
  237.1 0.6 dynamic_slice.9
  237.7 0.6 iota_add_fusion.2
  238.3 6.1 %fusion.95 = f32[2,512,512]{2,1,0:T(8,128)} fusion(f32[2,512,512]{2,1,0:T(8,128)} %get-tuple-element.107, s32[]{:T(128)} %get-tuple-element.106, f32[1544,512]{1,0:T(8,128)} %get-tuple-element.116, s32[1544]{0:T(1024)S(1)} %get-tuple-element.114, s32[512]{0:T(512)S(1)} %iota_add_fusion.2), kind=kOutput, calls=%fused_computation.7.clone.1 | convolution fusion | flops 4857794560 | bytes 4219424 | tf_op jit(solution)/shard_map/while/body/eval_jaxpr/dot_general | solution.py:522
  244.4 0.6 dynamic_slice.9
  245.0 0.6 iota_add_fusion.2
  245.6 6.1 %fusion.95 = f32[2,512,512]{2,1,0:T(8,128)} fusion(f32[2,512,512]{2,1,0:T(8,128)} %get-tuple-element.107, s32[]{:T(128)} %get-tuple-element.106, f32[1544,512]{1,0:T(8,128)} %get-tuple-element.116, s32[1544]{0:T(1024)S(1)} %get-tuple-element.114, s32[512]{0:T(512)S(1)} %iota_add_fusion.2), kind=kOutput, calls=%fused_computation.7.clone.1 | convolution fusion | flops 4857794560 | bytes 4219424 | tf_op jit(solution)/shard_map/while/body/eval_jaxpr/dot_general | solution.py:522
  251.8 53.8 %shard_map.95 = f32[1024,512]{1,0:T(8,128)} custom-call(f32[1024,512]{1,0:T(8,128)} %bitcast.98), custom_call_target="tpu_custom_call" | custom-call | flops 1048576 | bytes 8388608 | tf_op jit(solution)/shard_map/pallas_call | solution.py:167
  305.6 3.2 %copy.80 = f32[1024,512]{1,0:T(8,128)} copy(f32[1024,512]{1,0:T(8,128)} %shard_map.95) | data formatting | bytes 4194304
  308.8 2.0 copy.81
  (43 shorter events, 0.6 us)
Async XLA Ops:
  7.2 1.5 copy-start
  7.2 7.2 %copy-start.1 = (s32[512]{0:T(512)S(1)}, s32[512]{0:T(512)}, u32[]{:S(2)}) copy-start(s32[512]{0:T(512)} %param.14) | copy-start | bytes 6148
  7.2 86.9 %all-gather.2.cloned.1.call-start = ((), (), s32[]{:S(2)}) async-start(), calls=%async_computation.3 | async-start | bytes 2129920 | tf_op jit(solution)/shard_map/all_gather | solution.py:426
  14.4 20.7 %copy-start.10 = (s32[32]{0:T(128)S(1)}, s32[32]{0:T(128)}, u32[]{:S(2)}) copy-start(s32[32]{0:T(128)} %param.15) | copy-start | bytes 388
  22.1 22.4 %all-to-all-start = ((s32[64,1,16]{2,1,0:T(1,128)}), s32[64,1,16]{2,1,0:T(1,128)S(1)}, u32[]{:S(2)}, u32[]{:S(2)}) async-start(s32[64,1,16]{2,1,0:T(1,128)} %bitcast.7), calls=%async_computation | async-start | bytes 65536 | tf_op jit(solution)/shard_map/all_to_all | solution.py:419
  48.1 4.9 %copy-start.8 = (s32[512]{0:T(512)S(1)}, s32[512]{0:T(512)}, u32[]{:S(2)}) copy-start(s32[512]{0:T(512)} %param.12) | copy-start | bytes 6148
  48.1 5.0 %copy-start.6 = (s32[512,1]{0,1:T(1,128)S(1)}, s32[512,1]{0,1:T(1,128)}, u32[]{:S(2)}) copy-start(s32[512,1]{0,1:T(1,128)} %param.13) | copy-start | bytes 6148
  48.1 5.0 %copy-start.9 = (s32[512]{0:T(512)S(1)}, s32[512]{0:T(512)}, u32[]{:S(2)}) copy-start(s32[512]{0:T(512)} %param.11) | copy-start | bytes 6148
  48.1 35.8 %all-to-all-start.1 = ((bf16[64,16,512]{2,1,0:T(8,128)(2,1)}), bf16[64,16,512]{2,1,0:T(8,128)(2,1)S(1)}, u32[]{:S(2)}, u32[]{:S(2)}) async-start(bf16[64,16,512]{2,1,0:T(8,128)(2,1)} %bitcast.14), calls=%async_computation.1 | async-start | bytes 2097152 | tf_op jit(solution)/shard_map/all_to_all | solution.py:423
  53.0 1.6 copy-start.3
  103.8 128.2 %all-to-all-start.2 = ((bf16[64,16,640]{2,1,0:T(8,128)(2,1)}), bf16[64,16,640]{2,1,0:T(8,128)(2,1)}, u32[]{:S(2)}, u32[]{:S(2)}) async-start(bf16[64,16,640]{2,1,0:T(8,128)(2,1)} %bitcast.19), calls=%async_computation.2 | async-start | bytes 2621440 | tf_op jit(solution)/shard_map/all_to_all | solution.py:489
  117.0 2.5 copy-start.2
  228.7 1.8 copy-start.4
  232.0 3.0 copy-start.7
  305.6 3.2 %copy-start.5 = (f32[2048,512]{1,0:T(8,128)S(1)}, f32[2048,512]{1,0:T(8,128)}, u32[]{:S(2)}) copy-start(f32[2048,512]{1,0:T(8,128)} %get-tuple-element.40) | copy-start | bytes 12582916
Sparse Core Ops, SparseCore 0:
  10.8 83.2 all-gather.1

commit v3 on v2

--- a/solution.py
+++ b/solution.py
@@ -413,16 +413,14 @@
     )
     filled = jnp.sum(slot_match, axis=1) > 0
     source = jnp.sum(slot_match * jnp.arange(edge_count, dtype=jnp.int32)[None, :], axis=1)
-    send_ids = jnp.where(filled, jnp.take(tail_local, source, axis=0), 0).reshape(
-        part_count, capacity
-    )
+    send_ids = jnp.sum(slot_match * tail_local[None, :], axis=1).reshape(part_count, capacity)
     recv_ids = lax.all_to_all(send_ids, "dom", split_axis=0, concat_axis=0, tiled=True)
     looked_up = pick_rows(entities, recv_ids.reshape(-1)).reshape(
         part_count, capacity, columns
     )
     returned = lax.all_to_all(looked_up, "dom", split_axis=0, concat_axis=0, tiled=True)
     tail_embed = pick_rows(returned.reshape(slot_count, columns), slot_index)
-    own_negs = jnp.take(entities, neg_local, axis=0)
+    own_negs = pick_rows(entities, neg_local)
     negatives = lax.all_gather(own_negs, "dom", axis=0, tiled=True)
     positive = (
         jnp.sum(queries.astype(jnp.float32) * tail_embed.astype(jnp.float32), axis=1) * factor

time: 318 us -> 318 us (level)
  local copies, waits for them, and re-layouts: 19.5 us -> 14.3 us
  waiting for transfers between devices: 45.2 us -> 50.3 us
    gather x3 -> x0, local copies, waits for them, and re-layouts: 7.57 us -> none  [the longest x2 6.94 us: local(): jnp.take(tail_local, source, axis=0)]
    all_gather x1, waiting for transfers between devices: 8.66 us -> 15.6 us  [local(): negatives = lax.all_gather(own_negs, 'dom', axis=0, tiled=True)]
    unnamed x24 -> x20, local copies, waits for them, and re-layouts: 6.12 us -> 7.28 us
  transfers between devices with their start and end apart: 4 -> 4, of which waited for: 3 -> 3; matrix products, arithmetic and copies ran while one was open for 11% -> 9% of each run, Pallas kernels for 33% -> 33%
where the time goes in v3:
time: 318 us; the launch traced here: 317 us
  Pallas kernels  159 us (50%)
  waiting for transfers between devices  50.3 us (16%)
  matrix products  35.6 us (11%)
  starting transfers between devices  25.9 us (8%)
  other arithmetic  17.5 us (6%)
  between operations  14.4 us (5%)
  local copies, waits for them, and re-layouts  14.3 us (4%)
    pallas_call x1, Pallas kernels, lane_reduce(): pl.pallas_call(functools.partial(_lane_kernel, tuple(lanes), (n_dom, n_re...  105 us
    pallas_call x1, Pallas kernels, tree_reduce(): pl.pallas_call(functools.partial(_reduce_kernel, tuple(rs), tuple(ag), (n...  53.7 us
    all_to_all x1, waiting for transfers between devices, local(): lax.all_to_all(looked_up, 'dom', split_axis=0, concat_axis=0, tiled=True)  26.1 us
    all_gather x1, waiting for transfers between devices, local(): negatives = lax.all_gather(own_negs, 'dom', axis=0, tiled=True)  15.6 us
    all_to_all x1, starting transfers between devices, local(): lax.all_to_all(send_ids, 'dom', split_axis=0, concat_axis=0, tiled=True)  13 us
    dot_general x2, matrix products, add_block(): jnp.dot(hot, target_rows, precision=lax.Precision.HIGHEST, preferred_elem...  12.2 us
    all_to_all x1, waiting for transfers between devices, local(): lax.all_to_all(send_ids, 'dom', split_axis=0, concat_axis=0, tiled=True)  8.55 us
    all_to_all x1, starting transfers between devices, local(): lax.all_to_all(pack_send.reshape(part_count, capacity, pack.shape[1]), 'd...  7.94 us
  transfers between devices with their start and end apart: 4, of which 3 were waited for; matrix products, arithmetic and copies ran while one was open for 9% of the time, Pallas kernels for 33%

profile of v3, /device:TPU:1, one launch (start us, length us, event | category | flops | bytes accessed | tf_op | source)
XLA Modules:
  0.0 317.1 jit_solution(13702221393127528595)
XLA Ops:
  7.2 0.0 all-gather.2.cloned.1.call-start
  7.2 1.2 copy-done
  8.4 1.6 convolution_convert_fusion.1
  10.0 0.7 fusion.58
  10.7 1.2 reduce-window.6
  11.9 0.2 slice_reduce_fusion
  12.2 0.8 fusion.57
  13.0 0.7 multiply_add_fusion.1
  13.7 1.0 select_reduce_fusion
  14.6 0.7 all_to_all.12
  15.3 13.0 %all-to-all-start = ((s32[64,1,16]{2,1,0:T(1,128)}), s32[64,1,16]{2,1,0:T(1,128)S(1)}, u32[]{:S(2)}, u32[]{:S(2)}) async-start(s32[64,1,16]{2,1,0:T(1,128)} %bitcast.5), calls=%async_computation | async-start | bytes 65536 | tf_op jit(solution)/shard_map/all_to_all | solution.py:417
  28.3 0.7 dynamic_slice.7
  29.1 8.6 %all-to-all-done = s32[64,1,16]{2,1,0:T(1,128)S(1)} async-done(((s32[64,1,16]{2,1,0:T(1,128)}), s32[64,1,16]{2,1,0:T(1,128)S(1)}, u32[]{:S(2)}, u32[]{:S(2)}) %all-to-all-start) | async-done | bytes 4128 | tf_op jit(solution)/shard_map/all_to_all | solution.py:417
  37.6 0.5 broadcast.174
  38.1 0.7 reduce.7
  38.9 0.1 reshape.171
  38.9 2.3 fusion.15
  41.2 4.9 %all-to-all-start.1 = ((bf16[64,16,512]{2,1,0:T(8,128)(2,1)}), bf16[64,16,512]{2,1,0:T(8,128)(2,1)S(1)}, u32[]{:S(2)}, u32[]{:S(2)}) async-start(bf16[64,16,512]{2,1,0:T(8,128)(2,1)} %bitcast.12), calls=%async_computation.1 | async-start | bytes 2097152 | tf_op jit(solution)/shard_map/all_to_all | solution.py:421
  46.2 0.8 fusion.19
  47.0 0.8 copy-done.2
  47.7 0.5 fusion.33
  48.2 0.5 convolution_add_fusion.5
  48.7 0.5 convolution_add_fusion.4
  49.2 0.5 fusion.20
  49.7 26.1 %all-to-all-done.1 = bf16[64,16,512]{2,1,0:T(8,128)(2,1)S(1)} async-done(((bf16[64,16,512]{2,1,0:T(8,128)(2,1)}), bf16[64,16,512]{2,1,0:T(8,128)(2,1)S(1)}, u32[]{:S(2)}, u32[]{:S(2)}) %all-to-all-start.1) | async-done | bytes 1048608 | tf_op jit(solution)/shard_map/all_to_all | solution.py:421
  75.8 1.5 fusion.21
  77.4 15.6 %all-gather.2.cloned.1.call-done = bf16[2048,512]{1,0:T(8,128)(2,1)} async-done(((bf16[32,512]{1,0:T(8,128)(2,1)}), bf16[2048,512]{1,0:T(8,128)(2,1)}) %all-gather.2.cloned.1.call-update) | async-done | bytes 2097168 | tf_op jit(solution)/shard_map/all_gather | solution.py:424
  93.0 3.0 multiply_reduce_fusion
  96.0 0.8 fusion.11
  96.8 0.6 add_subtract_fusion
  97.4 2.1 divide_convert_fusion
  99.6 0.2 copy.58
  99.8 0.2 copy.59
  100.0 0.2 copy.60
  100.2 0.4 concatenate.11
  100.6 2.1 convolution_convert_fusion
  102.7 7.9 %all-to-all-start.2 = ((bf16[64,16,640]{2,1,0:T(8,128)(2,1)}), bf16[64,16,640]{2,1,0:T(8,128)(2,1)}, u32[]{:S(2)}, u32[]{:S(2)}) async-start(bf16[64,16,640]{2,1,0:T(8,128)(2,1)} %bitcast.17), calls=%async_computation.2 | async-start | bytes 2621440 | tf_op jit(solution)/shard_map/all_to_all | solution.py:487
  110.7 3.6 %fusion.17 = bf16[512,512]{1,0:T(8,128)(2,1)S(1)} fusion(bf16[512,2048]{1,0:T(8,128)(2,1)} %divide_convert_fusion, bf16[2048,512]{1,0:T(8,128)(2,1)} %all-gather.2.cloned.1.call-done, bf16[512,512]{1,0:T(8,128)(2,1)} %get-tuple-element.66, f32[512]{0:T(512)S(1)} %get-tuple-element.54), kind=kOutput, calls=%fused_computation.41 | convolution fusion | flops 1075052544 | bytes 5244928 | tf_op jit(solution)/shard_map/dot_general | solution.py:441
  114.2 0.6 convolution_bitcast_fusion.1
  114.8 0.6 convolution_bitcast_fusion.2
  115.3 0.6 convolution_bitcast_fusion.3
  115.9 0.6 convolution_bitcast_fusion
  116.5 2.5 pad_maximum_fusion
  118.9 1.3 convolution_multiply_fusion
  120.2 2.6 copy.61
  122.8 105.5 %shard_map.94 = (f32[2048,512]{1,0:T(8,128)}, f32[8,512]{1,0:T(8,128)}) custom-call(f32[2048,512]{1,0:T(8,128)} %bitcast.94, f32[2048,512]{1,0:T(8,128)} %bitcast.95), custom_call_target="tpu_custom_call" | custom-call | flops 8388608 | bytes 33554432 | tf_op jit(solution)/shard_map/pallas_call | solution.py:368
  228.3 1.7 fusion.31
  230.0 0.1 copy-done.3
  230.0 0.5 convolution_add_fusion.2
  230.5 0.5 convolution_add_fusion.1
  231.0 0.5 convolution_add_fusion
  231.6 1.6 add_reduce_fusion
  233.1 1.4 convert_multiply_fusion
  234.6 2.1 pad_maximum_fusion.1
  236.6 14.7 %while.10 = (s32[]{:T(128)}, f32[2,512,512]{2,1,0:T(8,128)}, s32[1544]{0:T(1024)S(1)}, s32[2]{0:T(128)S(1)}, f32[1544,512]{1,0:T(8,128)}, /*index=5*/s32[]{:T(128)}) while((s32[]{:T(128)}, f32[2,512,512]{2,1,0:T(8,128)}, s32[1544]{0:T(1024)S(1)}, s32[2]{0:T(128)S(1)}, f32[1544,512]{1,0:T(8,128)}, /*index=5*/s32[]{:T(128)}) %tuple.34), condition=%wide.region_8.9_spmd, body=%wide.region_7.8_spmd.sunk | while | flops 4857795072 | bytes 4221557 | solution.py:524
  236.6 0.6 dynamic_slice.9
  237.2 0.6 iota_add_fusion.2
  237.9 6.1 %fusion.97 = f32[2,512,512]{2,1,0:T(8,128)} fusion(f32[2,512,512]{2,1,0:T(8,128)} %get-tuple-element.105, s32[]{:T(128)} %get-tuple-element.104, f32[1544,512]{1,0:T(8,128)} %get-tuple-element.114, s32[1544]{0:T(1024)S(1)} %get-tuple-element.112, s32[512]{0:T(512)S(1)} %iota_add_fusion.2), kind=kOutput, calls=%fused_computation.5.clone.1 | convolution fusion | flops 4857794560 | bytes 4219424 | tf_op jit(solution)/shard_map/while/body/eval_jaxpr/dot_general | solution.py:520
  244.0 0.6 dynamic_slice.9
  244.6 0.6 iota_add_fusion.2
  245.2 6.1 %fusion.97 = f32[2,512,512]{2,1,0:T(8,128)} fusion(f32[2,512,512]{2,1,0:T(8,128)} %get-tuple-element.105, s32[]{:T(128)} %get-tuple-element.104, f32[1544,512]{1,0:T(8,128)} %get-tuple-element.114, s32[1544]{0:T(1024)S(1)} %get-tuple-element.112, s32[512]{0:T(512)S(1)} %iota_add_fusion.2), kind=kOutput, calls=%fused_computation.5.clone.1 | convolution fusion | flops 4857794560 | bytes 4219424 | tf_op jit(solution)/shard_map/while/body/eval_jaxpr/dot_general | solution.py:520
  251.3 53.7 %shard_map.95 = f32[1024,512]{1,0:T(8,128)} custom-call(f32[1024,512]{1,0:T(8,128)} %bitcast.97), custom_call_target="tpu_custom_call" | custom-call | flops 1048576 | bytes 8388608 | tf_op jit(solution)/shard_map/pallas_call | solution.py:167
  305.0 3.2 %copy.80 = f32[1024,512]{1,0:T(8,128)} copy(f32[1024,512]{1,0:T(8,128)} %shard_map.95) | data formatting | bytes 4194304
  308.2 2.0 copy.81
  (28 shorter events, 0.2 us)
Async XLA Ops:
  7.2 1.2 copy-start
  7.2 85.8 %all-gather.2.cloned.1.call-start = ((), (), s32[]{:S(2)}) async-start(), calls=%async_computation.3 | async-start | bytes 2129920 | tf_op jit(solution)/shard_map/all_gather | solution.py:424
  15.3 22.3 %all-to-all-start = ((s32[64,1,16]{2,1,0:T(1,128)}), s32[64,1,16]{2,1,0:T(1,128)S(1)}, u32[]{:S(2)}, u32[]{:S(2)}) async-start(s32[64,1,16]{2,1,0:T(1,128)} %bitcast.5), calls=%async_computation | async-start | bytes 65536 | tf_op jit(solution)/shard_map/all_to_all | solution.py:417
  41.2 4.9 %copy-start.7 = (s32[512]{0:T(512)S(1)}, s32[512]{0:T(512)}, u32[]{:S(2)}) copy-start(s32[512]{0:T(512)} %param.12) | copy-start | bytes 6148
  41.2 5.0 %copy-start.5 = (s32[512,1]{0,1:T(1,128)S(1)}, s32[512,1]{0,1:T(1,128)}, u32[]{:S(2)}) copy-start(s32[512,1]{0,1:T(1,128)} %param.13) | copy-start | bytes 6148
  41.2 5.0 %copy-start.8 = (s32[512]{0:T(512)S(1)}, s32[512]{0:T(512)}, u32[]{:S(2)}) copy-start(s32[512]{0:T(512)} %param.11) | copy-start | bytes 6148
  41.2 34.6 %all-to-all-start.1 = ((bf16[64,16,512]{2,1,0:T(8,128)(2,1)}), bf16[64,16,512]{2,1,0:T(8,128)(2,1)S(1)}, u32[]{:S(2)}, u32[]{:S(2)}) async-start(bf16[64,16,512]{2,1,0:T(8,128)(2,1)} %bitcast.12), calls=%async_computation.1 | async-start | bytes 2097152 | tf_op jit(solution)/shard_map/all_to_all | solution.py:421
  46.1 1.6 copy-start.2
  102.7 128.8 %all-to-all-start.2 = ((bf16[64,16,640]{2,1,0:T(8,128)(2,1)}), bf16[64,16,640]{2,1,0:T(8,128)(2,1)}, u32[]{:S(2)}, u32[]{:S(2)}) async-start(bf16[64,16,640]{2,1,0:T(8,128)(2,1)} %bitcast.17), calls=%async_computation.2 | async-start | bytes 2621440 | tf_op jit(solution)/shard_map/all_to_all | solution.py:487
  116.4 2.5 copy-start.1
  228.3 1.8 copy-start.3
  231.5 3.0 copy-start.6
  305.0 3.2 %copy-start.4 = (f32[2048,512]{1,0:T(8,128)S(1)}, f32[2048,512]{1,0:T(8,128)}, u32[]{:S(2)}) copy-start(f32[2048,512]{1,0:T(8,128)} %get-tuple-element.40) | copy-start | bytes 12582916
Sparse Core Ops, SparseCore 0:
  10.8 82.1 all-gather.1

commit v4 on v3

--- a/solution.py
+++ b/solution.py
@@ -510,7 +510,7 @@
     target_rows = jnp.concatenate(
         [head_grad, grad_recv.reshape(slot_count, columns), owned], axis=0
     )
-    block_rows = min(512, ent_dev)
+    block_rows = ent_dev
     block_count = ent_dev // block_rows
 
     def add_block(start):

time: 318 us -> 308 us (0.969)
  blocking collectives: 0 us -> 22.2 us
  starting transfers between devices: 25.9 us -> 13.5 us
  waiting for transfers between devices: 50.3 us -> 39.4 us
  other arithmetic: 17.5 us -> 14.2 us
    all_to_all x0 -> x1, blocking collectives: none -> 22.2 us  [local(): lax.all_to_all(send_ids, 'dom', split_axis=0, concat_axis=0, tiled=True)]
    all_to_all x1 -> x0, starting transfers between devices: 13 us -> none  [local(): lax.all_to_all(send_ids, 'dom', split_axis=0, concat_axis=0, tiled=True)]
    all_to_all x1 -> x0, waiting for transfers between devices: 8.55 us -> none  [local(): lax.all_to_all(send_ids, 'dom', split_axis=0, concat_axis=0, tiled=True)]
    dot_general x2 -> x1, matrix products: 12.2 us -> 7.27 us  [add_block(): jnp.dot(hot, target_rows, precision=lax.Precision.HIGHEST, preferred_elem...]
    unnamed x20 -> x26, local copies, waits for them, and re-layouts: 7.28 us -> 7.21 us
  transfers between devices with their start and end apart: 4 -> 3, of which waited for: 3 -> 2; matrix products, arithmetic and copies ran while one was open for 9% -> 10% of each run, Pallas kernels for 33% -> 34%
where the time goes in v4:
time: 308 us; the launch traced here: 307 us
  Pallas kernels  159 us (52%)
  waiting for transfers between devices  39.4 us (13%)
  matrix products  33 us (11%)
  blocking collectives  22.2 us (7%)
  between operations  14.4 us (5%)
  other arithmetic  14.2 us (5%)
  starting transfers between devices  13.5 us (4%)
  local copies, waits for them, and re-layouts  11.8 us (4%)
    pallas_call x1, Pallas kernels, lane_reduce(): pl.pallas_call(functools.partial(_lane_kernel, tuple(lanes), (n_dom, n_re...  105 us
    pallas_call x1, Pallas kernels, tree_reduce(): pl.pallas_call(functools.partial(_reduce_kernel, tuple(rs), tuple(ag), (n...  53.6 us
    all_to_all x1, waiting for transfers between devices, local(): lax.all_to_all(looked_up, 'dom', split_axis=0, concat_axis=0, tiled=True)  25 us
    all_to_all x1, blocking collectives, local(): lax.all_to_all(send_ids, 'dom', split_axis=0, concat_axis=0, tiled=True)  22.2 us
    all_gather x1, waiting for transfers between devices, local(): negatives = lax.all_gather(own_negs, 'dom', axis=0, tiled=True)  14.4 us
    all_to_all x1, starting transfers between devices, local(): lax.all_to_all(pack_send.reshape(part_count, capacity, pack.shape[1]), 'd...  7.84 us
    dot_general x4, matrix products, pick_rows(): jnp.dot(hot, table, preferred_element_type=jnp.float32).astype(table.dtype)  7.42 us
    dot_general x1, matrix products, add_block(): jnp.dot(hot, target_rows, precision=lax.Precision.HIGHEST, preferred_elem...  7.27 us
  transfers between devices with their start and end apart: 3, of which 2 were waited for; matrix products, arithmetic and copies ran while one was open for 10% of the time, Pallas kernels for 34%

profile of v4, /device:TPU:1, one launch (start us, length us, event | category | flops | bytes accessed | tf_op | source)
XLA Modules:
  0.0 307.2 jit_solution(14033575272245979078)
XLA Ops:
  7.2 0.0 copy-start
  7.2 0.0 all-gather.2.cloned.1.call-start
  7.2 1.2 copy-done
  8.4 1.6 convolution_convert_fusion.1
  10.0 0.0 all-gather.2.cloned.1.call-update
  10.0 0.7 fusion.55
  10.7 1.2 reduce-window.6
  11.9 0.2 slice_reduce_fusion
  12.2 0.8 fusion.54
  13.0 0.7 multiply_add_fusion.1
  13.7 1.0 select_reduce_fusion
  14.6 0.1 all_to_all.12
  14.7 22.2 %all_to_all.19 = s32[64,1,16]{2,1,0:T(1,128)S(1)} all-to-all(s32[64,1,16]{2,1,0:T(1,128)S(1)} %bitcast.84), channel_id=1, replica_groups=mesh['dom'=64,'rep'=4] {'dom'}, dimensions={0} | all-to-all | bytes 8192 | tf_op jit(solution)/shard_map/all_to_all | solution.py:417
  37.0 0.5 broadcast.166
  37.5 0.7 reduce.7
  38.2 0.1 reshape.167
  38.3 2.3 fusion.12
  40.6 5.7 %all-to-all-start.1 = ((bf16[64,16,512]{2,1,0:T(8,128)(2,1)}), bf16[64,16,512]{2,1,0:T(8,128)(2,1)}, u32[]{:S(2)}, u32[]{:S(2)}) async-start(bf16[64,16,512]{2,1,0:T(8,128)(2,1)} %bitcast.10), calls=%async_computation.1 | async-start | bytes 2097152 | tf_op jit(solution)/shard_map/all_to_all | solution.py:421
  46.2 0.0 copy-start.2
  46.3 0.1 dynamic_slice.6
  46.3 0.0 copy-done.7
  46.4 0.8 fusion.16
  47.1 0.0 copy-start.4
  47.1 0.7 copy-done.2
  47.8 0.5 fusion.30
  48.3 0.5 convolution_add_fusion.5
  48.8 0.5 convolution_add_fusion.4
  49.3 1.5 fusion.17
  50.9 25.0 %all-to-all-done.1 = bf16[64,16,512]{2,1,0:T(8,128)(2,1)} async-done(((bf16[64,16,512]{2,1,0:T(8,128)(2,1)}), bf16[64,16,512]{2,1,0:T(8,128)(2,1)}, u32[]{:S(2)}, u32[]{:S(2)}) %all-to-all-start.1) | async-done | bytes 1048608 | tf_op jit(solution)/shard_map/all_to_all | solution.py:421
  75.9 2.8 fusion.18
  78.7 14.4 %all-gather.2.cloned.1.call-done = bf16[2048,512]{1,0:T(8,128)(2,1)} async-done(((bf16[32,512]{1,0:T(8,128)(2,1)}), bf16[2048,512]{1,0:T(8,128)(2,1)}) %all-gather.2.cloned.1.call-update) | async-done | bytes 2097168 | tf_op jit(solution)/shard_map/all_gather | solution.py:424
  93.1 3.0 multiply_reduce_fusion
  96.1 0.8 fusion.2
  96.9 0.6 add_subtract_fusion
  97.5 2.2 divide_convert_fusion
  99.7 0.2 copy.71
  99.9 0.2 copy.72
  100.1 0.2 copy.73
  100.3 0.4 concatenate.11
  100.7 2.1 convolution_convert_fusion
  102.8 7.8 %all-to-all-start.2 = ((bf16[64,16,640]{2,1,0:T(8,128)(2,1)}), bf16[64,16,640]{2,1,0:T(8,128)(2,1)}, u32[]{:S(2)}, u32[]{:S(2)}) async-start(bf16[64,16,640]{2,1,0:T(8,128)(2,1)} %bitcast.15), calls=%async_computation.2 | async-start | bytes 2621440 | tf_op jit(solution)/shard_map/all_to_all | solution.py:487
  110.6 3.6 %fusion.14 = bf16[512,512]{1,0:T(8,128)(2,1)S(1)} fusion(bf16[512,2048]{1,0:T(8,128)(2,1)} %divide_convert_fusion, bf16[2048,512]{1,0:T(8,128)(2,1)} %all-gather.2.cloned.1.call-done, bf16[512,512]{1,0:T(8,128)(2,1)} %get-tuple-element.40, f32[512]{0:T(512)S(1)} %get-tuple-element.28), kind=kOutput, calls=%fused_computation.41 | convolution fusion | flops 1075052544 | bytes 5244928 | tf_op jit(solution)/shard_map/dot_general | solution.py:441
  114.3 0.6 convolution_bitcast_fusion
  114.8 0.6 convolution_bitcast_fusion.1
  115.4 0.6 convolution_bitcast_fusion.2
  115.9 0.6 convolution_bitcast_fusion.3
  116.5 0.0 copy-start.1
  116.5 2.5 pad_maximum_fusion
  119.0 1.3 convolution_multiply_fusion
  120.3 2.6 copy.74
  122.9 105.0 %shard_map.94 = (f32[2048,512]{1,0:T(8,128)}, f32[8,512]{1,0:T(8,128)}) custom-call(f32[2048,512]{1,0:T(8,128)} %bitcast.81, f32[2048,512]{1,0:T(8,128)} %bitcast.82), custom_call_target="tpu_custom_call" | custom-call | flops 8388608 | bytes 33554432 | tf_op jit(solution)/shard_map/pallas_call | solution.py:368
  227.9 0.0 copy-start.3
  227.9 1.7 fusion.28
  229.6 0.1 copy-done.3
  229.6 0.5 convolution_add_fusion.2
  230.1 0.5 convolution_add_fusion.1
  230.6 0.5 convolution_add_fusion
  231.1 0.0 all-to-all-done.2
  231.1 1.6 add_reduce_fusion
  232.7 1.4 convert_multiply_fusion
  234.2 7.3 %fusion.x_ref = f32[1024,512]{1,0:T(8,128)} fusion(s32[1544]{0:T(1024)S(1)} %pad_add_fusion, f32[8,512]{1,0:T(8,128)S(1)} %copy-done.11, f32[1024,512]{1,0:T(8,128)S(1)} %convert_multiply_fusion, f32[512,512]{1,0:T(8,128)S(1)} %convolution_add_fusion), kind=kOutput, calls=%fused_computation.1 | convolution fusion | flops 9717170176 | bytes 5265440 | tf_op jit(solution)/shard_map/while/body/eval_jaxpr/dot_general | solution.py:520
  241.4 53.6 %shard_map.95 = f32[1024,512]{1,0:T(8,128)} custom-call(f32[1024,512]{1,0:T(8,128)} %fusion.x_ref), custom_call_target="tpu_custom_call" | custom-call | flops 1048576 | bytes 8388608 | tf_op jit(solution)/shard_map/pallas_call | solution.py:167
  295.1 3.2 %copy.84 = f32[1024,512]{1,0:T(8,128)} copy(f32[1024,512]{1,0:T(8,128)} %shard_map.95) | data formatting | bytes 4194304
  298.3 2.0 copy.85
  (24 shorter events, 0.1 us)
Async XLA Ops:
  7.2 1.2 copy-start
  7.2 85.9 %all-gather.2.cloned.1.call-start = ((), (), s32[]{:S(2)}) async-start(), calls=%async_computation.3 | async-start | bytes 2129920 | tf_op jit(solution)/shard_map/all_gather | solution.py:424
  40.6 5.7 %copy-start.10 = (s32[32]{0:T(128)S(1)}, s32[32]{0:T(128)}, u32[]{:S(2)}) copy-start(s32[32]{0:T(128)} %param.13) | copy-start | bytes 388
  40.6 5.8 %copy-start.8 = (s32[512]{0:T(512)S(1)}, s32[512]{0:T(512)}, u32[]{:S(2)}) copy-start(s32[512]{0:T(512)} %param.10) | copy-start | bytes 6148
  40.6 5.8 %copy-start.7 = (s32[512,1]{0,1:T(1,128)S(1)}, s32[512,1]{0,1:T(1,128)}, u32[]{:S(2)}) copy-start(s32[512,1]{0,1:T(1,128)} %param.11) | copy-start | bytes 6148
  40.6 5.8 %copy-start.9 = (s32[512]{0:T(512)S(1)}, s32[512]{0:T(512)}, u32[]{:S(2)}) copy-start(s32[512]{0:T(512)} %param.9) | copy-start | bytes 6148
  40.6 35.3 %all-to-all-start.1 = ((bf16[64,16,512]{2,1,0:T(8,128)(2,1)}), bf16[64,16,512]{2,1,0:T(8,128)(2,1)}, u32[]{:S(2)}, u32[]{:S(2)}) async-start(bf16[64,16,512]{2,1,0:T(8,128)(2,1)} %bitcast.10), calls=%async_computation.1 | async-start | bytes 2097152 | tf_op jit(solution)/shard_map/all_to_all | solution.py:421
  46.2 1.6 copy-start.2
  47.1 2.2 copy-start.4
  102.8 128.3 %all-to-all-start.2 = ((bf16[64,16,640]{2,1,0:T(8,128)(2,1)}), bf16[64,16,640]{2,1,0:T(8,128)(2,1)}, u32[]{:S(2)}, u32[]{:S(2)}) async-start(bf16[64,16,640]{2,1,0:T(8,128)(2,1)} %bitcast.15), calls=%async_computation.2 | async-start | bytes 2621440 | tf_op jit(solution)/shard_map/all_to_all | solution.py:487
  110.6 3.6 %copy-start.5 = (bf16[512,512]{1,0:T(8,128)(2,1)S(1)}, bf16[512,512]{1,0:T(8,128)(2,1)}, u32[]{:S(2)}) copy-start(bf16[512,512]{1,0:T(8,128)(2,1)} %copy-done.4) | copy-start | bytes 1572868
  116.5 2.5 copy-start.1
  227.9 1.8 copy-start.3
  231.1 3.0 copy-start.11
  295.1 3.2 %copy-start.6 = (f32[2048,512]{1,0:T(8,128)S(1)}, f32[2048,512]{1,0:T(8,128)}, u32[]{:S(2)}) copy-start(f32[2048,512]{1,0:T(8,128)} %get-tuple-element.24) | copy-start | bytes 12582916
Sparse Core Ops, SparseCore 0:
  10.8 82.2 all-gather.1

commit v5 on v4

--- a/solution.py
+++ b/solution.py
@@ -422,6 +422,9 @@
     tail_embed = pick_rows(returned.reshape(slot_count, columns), slot_index)
     own_negs = pick_rows(entities, neg_local)
     negatives = lax.all_gather(own_negs, "dom", axis=0, tiled=True)
+    rep_count = lax.axis_size("rep")
+    negatives = negatives.reshape(part_count // 8, 4, 2, rep_count, -1, columns)
+    negatives = negatives.transpose(2, 3, 1, 0, 4, 5).reshape(-1, columns)
     positive = (
         jnp.sum(queries.astype(jnp.float32) * tail_embed.astype(jnp.float32), axis=1) * factor
     )
@@ -496,8 +499,7 @@
     ) + pack_recv[:, columns + 2].astype(jnp.float32)
     grad_recv = recv_scale[:, None] * pack_recv[:, :columns].astype(jnp.float32)
     rep_count = lax.axis_size("rep")
-    neg_order = neg_grad.reshape(part_count // 8, 4, 2, rep_count, -1, columns)
-    neg_order = neg_order.transpose(2, 3, 1, 0, 4, 5).reshape(-1, columns)
+    neg_order = neg_grad
     orders = (("core", "x", "y", "z"), ("core", "y", "x", "z"))
     width = columns // len(orders)
     lanes = [(0, width * i, width, order, order[::-1]) for i, order in enumerate(orders)]

time: 308 us -> 309 us (level)
    unnamed x26 -> x28, local copies, waits for them, and re-layouts: 7.21 us -> 7.22 us
where the time goes in v5:
time: 309 us; the launch traced here: 308 us
  Pallas kernels  159 us (51%)
  waiting for transfers between devices  40.1 us (13%)
  matrix products  33.4 us (11%)
  blocking collectives  22.1 us (7%)
  between operations  14.4 us (5%)
  other arithmetic  14.2 us (5%)
  starting transfers between devices  13.4 us (4%)
  local copies, waits for them, and re-layouts  11 us (4%)
    pallas_call x1, Pallas kernels, lane_reduce(): pl.pallas_call(functools.partial(_lane_kernel, tuple(lanes), (n_dom, n_re...  106 us
    pallas_call x1, Pallas kernels, tree_reduce(): pl.pallas_call(functools.partial(_reduce_kernel, tuple(rs), tuple(ag), (n...  53.8 us
    all_to_all x1, waiting for transfers between devices, local(): lax.all_to_all(looked_up, 'dom', split_axis=0, concat_axis=0, tiled=True)  24.5 us
    all_to_all x1, blocking collectives, local(): lax.all_to_all(send_ids, 'dom', split_axis=0, concat_axis=0, tiled=True)  22.1 us
    all_gather x1, waiting for transfers between devices, local(): negatives = lax.all_gather(own_negs, 'dom', axis=0, tiled=True)  15.6 us
    all_to_all x1, starting transfers between devices, local(): lax.all_to_all(pack_send.reshape(part_count, capacity, pack.shape[1]), 'd...  7.65 us
    dot_general x4, matrix products, pick_rows(): jnp.dot(hot, table, preferred_element_type=jnp.float32).astype(table.dtype)  7.41 us
    dot_general x1, matrix products, add_block(): jnp.dot(hot, target_rows, precision=lax.Precision.HIGHEST, preferred_elem...  7.27 us
  transfers between devices with their start and end apart: 3, of which 2 were waited for; matrix products, arithmetic and copies ran while one was open for 10% of the time, Pallas kernels for 34%

profile of v5, /device:TPU:1, one launch (start us, length us, event | category | flops | bytes accessed | tf_op | source)
XLA Modules:
  0.0 308.0 jit_solution(5832669837823026186)
XLA Ops:
  7.2 0.0 copy-start
  7.2 0.0 all-gather.2.cloned.1.call-start
  7.2 1.2 copy-done
  8.4 1.6 convolution_convert_fusion.1
  10.0 0.0 all-gather.2.cloned.1.call-update
  10.0 0.7 fusion.55
  10.7 1.2 reduce-window.6
  11.9 0.2 slice_reduce_fusion
  12.2 0.8 fusion.54
  13.0 0.7 multiply_add_fusion.1
  13.7 1.0 select_reduce_fusion
  14.7 0.1 all_to_all.12
  14.7 22.1 %all_to_all.19 = s32[64,1,16]{2,1,0:T(1,128)S(1)} all-to-all(s32[64,1,16]{2,1,0:T(1,128)S(1)} %bitcast.85), channel_id=1, replica_groups=mesh['dom'=64,'rep'=4] {'dom'}, dimensions={0} | all-to-all | bytes 8192 | tf_op jit(solution)/shard_map/all_to_all | solution.py:417
  36.9 0.5 broadcast.166
  37.4 0.7 reduce.7
  38.1 0.1 reshape.167
  38.2 2.3 fusion.12
  40.5 5.7 %all-to-all-start.1 = ((bf16[64,16,512]{2,1,0:T(8,128)(2,1)}), bf16[64,16,512]{2,1,0:T(8,128)(2,1)}, u32[]{:S(2)}, u32[]{:S(2)}) async-start(bf16[64,16,512]{2,1,0:T(8,128)(2,1)} %bitcast.10), calls=%async_computation.1 | async-start | bytes 2097152 | tf_op jit(solution)/shard_map/all_to_all | solution.py:421
  46.2 0.0 copy-start.3
  46.2 0.1 dynamic_slice.6
  46.3 0.0 copy-done.9
  46.3 0.8 fusion.16
  47.1 0.7 copy-done.3
  47.8 0.5 fusion.30
  48.3 0.5 convolution_add_fusion.5
  48.8 0.5 convolution_add_fusion.4
  49.3 1.5 fusion.17
  50.8 24.5 %all-to-all-done.1 = bf16[64,16,512]{2,1,0:T(8,128)(2,1)} async-done(((bf16[64,16,512]{2,1,0:T(8,128)(2,1)}), bf16[64,16,512]{2,1,0:T(8,128)(2,1)}, u32[]{:S(2)}, u32[]{:S(2)}) %all-to-all-start.1) | async-done | bytes 1048608 | tf_op jit(solution)/shard_map/all_to_all | solution.py:421
  75.3 2.8 fusion.18
  78.1 15.6 %all-gather.2.cloned.1.call-done = bf16[2048,512]{1,0:T(8,128)(2,1)} async-done(((bf16[32,512]{1,0:T(8,128)(2,1)}), bf16[2048,512]{1,0:T(8,128)(2,1)}) %all-gather.2.cloned.1.call-update) | async-done | bytes 2097168 | tf_op jit(solution)/shard_map/all_gather | solution.py:424
  93.7 1.9 copy.70
  95.6 0.0 copy-start.2
  95.6 1.4 multiply_reduce_fusion
  97.0 0.8 fusion.2
  97.8 0.6 add_subtract_fusion
  98.4 2.2 divide_convert_fusion
  100.6 0.2 copy.71
  100.8 0.2 copy.72
  101.0 0.2 copy.73
  101.2 0.4 concatenate.11
  101.6 2.1 convolution_convert_fusion
  103.7 7.7 %all-to-all-start.2 = ((bf16[64,16,640]{2,1,0:T(8,128)(2,1)}), bf16[64,16,640]{2,1,0:T(8,128)(2,1)}, u32[]{:S(2)}, u32[]{:S(2)}) async-start(bf16[64,16,640]{2,1,0:T(8,128)(2,1)} %bitcast.19), calls=%async_computation.2 | async-start | bytes 2621440 | tf_op jit(solution)/shard_map/all_to_all | solution.py:490
  111.4 3.6 %fusion.14 = bf16[512,512]{1,0:T(8,128)(2,1)S(1)} fusion(bf16[512,2048]{1,0:T(8,128)(2,1)} %divide_convert_fusion, bf16[2048,512]{1,0:T(8,128)(2,1)} %bitcast.82, bf16[512,512]{1,0:T(8,128)(2,1)} %get-tuple-element.40, f32[512]{0:T(512)S(1)} %get-tuple-element.28), kind=kOutput, calls=%fused_computation.41 | convolution fusion | flops 1075052544 | bytes 5244928 | tf_op jit(solution)/shard_map/dot_general | solution.py:444
  115.0 0.6 convolution_bitcast_fusion
  115.6 0.6 convolution_bitcast_fusion.1
  116.1 0.6 convolution_bitcast_fusion.2
  116.7 0.6 convolution_bitcast_fusion.3
  117.2 0.0 copy-start.1
  117.2 2.5 pad_maximum_fusion
  119.7 3.3 %convolution_multiply_fusion.refs_1_ = f32[2048,512]{1,0:T(8,128)} fusion(bf16[512,2048]{1,0:T(8,128)(2,1)S(1)} %copy-done.1, bf16[512,512]{1,0:T(8,128)(2,1)S(1)} %fusion.17), kind=kOutput, calls=%fused_computation.10 | convolution fusion | flops 1074790400 | bytes 6815744 | tf_op jit(solution)/shard_map/dot_general | solution.py:471
  123.0 105.5 %shard_map.94 = (f32[2048,512]{1,0:T(8,128)}, f32[8,512]{1,0:T(8,128)}) custom-call(f32[2048,512]{1,0:T(8,128)} %bitcast.80, f32[2048,512]{1,0:T(8,128)} %convolution_multiply_fusion.refs_1_), custom_call_target="tpu_custom_call" | custom-call | flops 8388608 | bytes 33554432 | tf_op jit(solution)/shard_map/pallas_call | solution.py:368
  228.5 0.0 copy-start.4
  228.5 1.7 fusion.28
  230.2 0.1 copy-done.4
  230.3 0.5 convolution_add_fusion.2
  230.7 0.5 convolution_add_fusion.1
  231.2 0.5 convolution_add_fusion
  231.8 0.0 all-to-all-done.2
  231.8 1.6 add_reduce_fusion
  233.3 1.4 convert_multiply_fusion
  234.8 7.3 %fusion.x_ref = f32[1024,512]{1,0:T(8,128)} fusion(s32[1544]{0:T(1024)S(1)} %pad_add_fusion, f32[8,512]{1,0:T(8,128)S(1)} %copy-done.12, f32[1024,512]{1,0:T(8,128)S(1)} %convert_multiply_fusion, f32[512,512]{1,0:T(8,128)S(1)} %convolution_add_fusion), kind=kOutput, calls=%fused_computation.1 | convolution fusion | flops 9717170176 | bytes 5265440 | tf_op jit(solution)/shard_map/while/body/eval_jaxpr/dot_general | solution.py:522
  242.1 53.8 %shard_map.95 = f32[1024,512]{1,0:T(8,128)} custom-call(f32[1024,512]{1,0:T(8,128)} %fusion.x_ref), custom_call_target="tpu_custom_call" | custom-call | flops 1048576 | bytes 8388608 | tf_op jit(solution)/shard_map/pallas_call | solution.py:167
  295.9 3.2 %copy.83 = f32[1024,512]{1,0:T(8,128)} copy(f32[1024,512]{1,0:T(8,128)} %shard_map.95) | data formatting | bytes 4194304
  299.1 2.0 copy.84
  (26 shorter events, 0.1 us)
Async XLA Ops:
  7.2 1.2 copy-start
  7.2 86.5 %all-gather.2.cloned.1.call-start = ((), (), s32[]{:S(2)}) async-start(), calls=%async_computation.3 | async-start | bytes 2129920 | tf_op jit(solution)/shard_map/all_gather | solution.py:424
  40.5 5.7 %copy-start.11 = (s32[32]{0:T(128)S(1)}, s32[32]{0:T(128)}, u32[]{:S(2)}) copy-start(s32[32]{0:T(128)} %param.13) | copy-start | bytes 388
  40.5 5.8 %copy-start.9 = (s32[512]{0:T(512)S(1)}, s32[512]{0:T(512)}, u32[]{:S(2)}) copy-start(s32[512]{0:T(512)} %param.10) | copy-start | bytes 6148
  40.5 5.8 %copy-start.8 = (s32[512,1]{0,1:T(1,128)S(1)}, s32[512,1]{0,1:T(1,128)}, u32[]{:S(2)}) copy-start(s32[512,1]{0,1:T(1,128)} %param.11) | copy-start | bytes 6148
  40.5 5.8 %copy-start.10 = (s32[512]{0:T(512)S(1)}, s32[512]{0:T(512)}, u32[]{:S(2)}) copy-start(s32[512]{0:T(512)} %param.9) | copy-start | bytes 6148
  40.5 34.8 %all-to-all-start.1 = ((bf16[64,16,512]{2,1,0:T(8,128)(2,1)}), bf16[64,16,512]{2,1,0:T(8,128)(2,1)}, u32[]{:S(2)}, u32[]{:S(2)}) async-start(bf16[64,16,512]{2,1,0:T(8,128)(2,1)} %bitcast.10), calls=%async_computation.1 | async-start | bytes 2097152 | tf_op jit(solution)/shard_map/all_to_all | solution.py:421
  46.2 1.6 copy-start.3
  47.1 2.2 copy-start.5
  95.6 1.4 copy-start.2
  103.7 128.1 %all-to-all-start.2 = ((bf16[64,16,640]{2,1,0:T(8,128)(2,1)}), bf16[64,16,640]{2,1,0:T(8,128)(2,1)}, u32[]{:S(2)}, u32[]{:S(2)}) async-start(bf16[64,16,640]{2,1,0:T(8,128)(2,1)} %bitcast.19), calls=%async_computation.2 | async-start | bytes 2621440 | tf_op jit(solution)/shard_map/all_to_all | solution.py:490
  111.4 3.6 %copy-start.6 = (bf16[512,512]{1,0:T(8,128)(2,1)S(1)}, bf16[512,512]{1,0:T(8,128)(2,1)}, u32[]{:S(2)}) copy-start(bf16[512,512]{1,0:T(8,128)(2,1)} %copy-done.5) | copy-start | bytes 1572868
  117.2 2.5 copy-start.1
  228.5 1.8 copy-start.4
  231.7 3.0 copy-start.12
  295.8 3.2 %copy-start.7 = (f32[2048,512]{1,0:T(8,128)S(1)}, f32[2048,512]{1,0:T(8,128)}, u32[]{:S(2)}) copy-start(f32[2048,512]{1,0:T(8,128)} %get-tuple-element.24) | copy-start | bytes 12582916
Sparse Core Ops, SparseCore 0:
  11.4 82.2 all-gather.1

commit v6 on v4

--- a/solution.py
+++ b/solution.py
@@ -508,7 +508,10 @@
     neg_ids = lax.dynamic_slice_in_dim(neg_local, lax.axis_index("rep") * neg_rows, neg_rows)
     target_ids = jnp.concatenate([head_local, recv_ids.reshape(-1), neg_ids])
     target_rows = jnp.concatenate(
-        [head_grad, grad_recv.reshape(slot_count, columns), owned], axis=0
+        [head_grad, pack_recv[:, :columns].astype(jnp.float32), owned], axis=0
+    )
+    target_weights = jnp.concatenate(
+        [jnp.ones((edge_count,), jnp.float32), recv_scale, jnp.ones((owned.shape[0],), jnp.float32)]
     )
     block_rows = ent_dev
     block_count = ent_dev // block_rows
@@ -516,7 +519,7 @@
     def add_block(start):
         hot = (
             target_ids[None, :] == (start + jnp.arange(block_rows, dtype=jnp.int32))[:, None]
-        ).astype(jnp.float32)
+        ).astype(jnp.float32) * target_weights[None, :]
         return jnp.dot(
             hot, target_rows, precision=lax.Precision.HIGHEST, preferred_element_type=jnp.float32
         )

time: 308 us -> 476 us (1.55)
  matrix products: 33 us -> 201 us
    dot_general x1, matrix products: 7.27 us -> 175 us  [add_block(): jnp.dot(hot, target_rows, precision=lax.Precision.HIGHEST, preferred_elem...]
  transfers between devices with their start and end apart: 3 -> 3, of which waited for: 2 -> 2; matrix products, arithmetic and copies ran while one was open for 10% -> 6% of each run, Pallas kernels for 34% -> 22%
where the time goes in v6:
time: 476 us; the launch traced here: 475 us
  matrix products  201 us (42%)
  Pallas kernels  159 us (33%)
  waiting for transfers between devices  39.4 us (8%)
  blocking collectives  22.2 us (5%)
  between operations  14.4 us (3%)
  other arithmetic  14.3 us (3%)
  starting transfers between devices  13.5 us (3%)
  local copies, waits for them, and re-layouts  11.8 us (2%)
    dot_general x1, matrix products, add_block(): jnp.dot(hot, target_rows, precision=lax.Precision.HIGHEST, preferred_elem...  175 us
    pallas_call x1, Pallas kernels, lane_reduce(): pl.pallas_call(functools.partial(_lane_kernel, tuple(lanes), (n_dom, n_re...  105 us
    pallas_call x1, Pallas kernels, tree_reduce(): pl.pallas_call(functools.partial(_reduce_kernel, tuple(rs), tuple(ag), (n...  53.6 us
    all_to_all x1, waiting for transfers between devices, local(): lax.all_to_all(looked_up, 'dom', split_axis=0, concat_axis=0, tiled=True)  25 us
    all_to_all x1, blocking collectives, local(): lax.all_to_all(send_ids, 'dom', split_axis=0, concat_axis=0, tiled=True)  22.2 us
    all_gather x1, waiting for transfers between devices, local(): negatives = lax.all_gather(own_negs, 'dom', axis=0, tiled=True)  14.4 us
  transfers between devices with their start and end apart: 3, of which 2 were waited for; matrix products, arithmetic and copies ran while one was open for 6% of the time, Pallas kernels for 22%

profile of v6, /device:TPU:1, one launch (start us, length us, event | category | flops | bytes accessed | tf_op | source)
XLA Modules:
  0.0 475.1 jit_solution(414846643902852478)
XLA Ops:
  7.2 0.0 copy-start
  7.2 0.0 all-gather.2.cloned.1.call-start
  7.2 1.2 copy-done
  8.4 1.6 convolution_convert_fusion.1
  10.0 0.0 all-gather.2.cloned.1.call-update
  10.0 0.7 fusion.58
  10.7 1.2 reduce-window.6
  11.9 0.2 slice_reduce_fusion
  12.2 0.8 fusion.57
  13.0 0.7 multiply_add_fusion.1
  13.7 1.0 select_reduce_fusion
  14.6 0.1 all_to_all.12
  14.7 22.2 %all_to_all.19 = s32[64,1,16]{2,1,0:T(1,128)S(1)} all-to-all(s32[64,1,16]{2,1,0:T(1,128)S(1)} %bitcast.84), channel_id=1, replica_groups=mesh['dom'=64,'rep'=4] {'dom'}, dimensions={0} | all-to-all | bytes 8192 | tf_op jit(solution)/shard_map/all_to_all | solution.py:417
  37.0 0.5 broadcast.182
  37.5 0.7 reduce.7
  38.2 0.1 reshape.173
  38.3 2.3 fusion.15
  40.6 5.7 %all-to-all-start.1 = ((bf16[64,16,512]{2,1,0:T(8,128)(2,1)}), bf16[64,16,512]{2,1,0:T(8,128)(2,1)}, u32[]{:S(2)}, u32[]{:S(2)}) async-start(bf16[64,16,512]{2,1,0:T(8,128)(2,1)} %bitcast.10), calls=%async_computation.1 | async-start | bytes 2097152 | tf_op jit(solution)/shard_map/all_to_all | solution.py:421
  46.2 0.0 copy-start.2
  46.3 0.1 dynamic_slice.6
  46.3 0.0 copy-done.8
  46.4 0.8 fusion.19
  47.1 0.7 copy-done.2
  47.8 0.5 fusion.33
  48.3 0.5 convolution_add_fusion.5
  48.8 0.5 convolution_add_fusion.4
  49.3 1.5 fusion.20
  50.9 25.0 %all-to-all-done.1 = bf16[64,16,512]{2,1,0:T(8,128)(2,1)} async-done(((bf16[64,16,512]{2,1,0:T(8,128)(2,1)}), bf16[64,16,512]{2,1,0:T(8,128)(2,1)}, u32[]{:S(2)}, u32[]{:S(2)}) %all-to-all-start.1) | async-done | bytes 1048608 | tf_op jit(solution)/shard_map/all_to_all | solution.py:421
  75.9 2.8 fusion.21
  78.7 14.4 %all-gather.2.cloned.1.call-done = bf16[2048,512]{1,0:T(8,128)(2,1)} async-done(((bf16[32,512]{1,0:T(8,128)(2,1)}), bf16[2048,512]{1,0:T(8,128)(2,1)}) %all-gather.2.cloned.1.call-update) | async-done | bytes 2097168 | tf_op jit(solution)/shard_map/all_gather | solution.py:424
  93.1 3.0 multiply_reduce_fusion
  96.1 0.8 fusion.3
  96.9 0.6 add_subtract_fusion
  97.5 2.2 divide_convert_fusion
  99.7 0.2 copy.71
  99.9 0.2 copy.72
  100.1 0.2 copy.73
  100.3 0.4 concatenate.14
  100.7 2.1 convolution_convert_fusion
  102.8 7.8 %all-to-all-start.2 = ((bf16[64,16,640]{2,1,0:T(8,128)(2,1)}), bf16[64,16,640]{2,1,0:T(8,128)(2,1)}, u32[]{:S(2)}, u32[]{:S(2)}) async-start(bf16[64,16,640]{2,1,0:T(8,128)(2,1)} %bitcast.15), calls=%async_computation.2 | async-start | bytes 2621440 | tf_op jit(solution)/shard_map/all_to_all | solution.py:487
  110.6 3.6 fusion.17
  114.3 0.0 copy-done.5
  114.3 0.6 convolution_bitcast_fusion.1
  114.8 0.6 convolution_bitcast_fusion.2
  115.4 0.6 convolution_bitcast_fusion.3
  115.9 0.6 convolution_bitcast_fusion
  116.5 0.0 copy-start.1
  116.5 2.5 pad_maximum_fusion
  119.0 1.3 convolution_multiply_fusion
  120.3 2.6 copy.74
  122.9 105.0 %shard_map.94 = (f32[2048,512]{1,0:T(8,128)}, f32[8,512]{1,0:T(8,128)}) custom-call(f32[2048,512]{1,0:T(8,128)} %bitcast.81, f32[2048,512]{1,0:T(8,128)} %bitcast.82), custom_call_target="tpu_custom_call" | custom-call | flops 8388608 | bytes 33554432 | tf_op jit(solution)/shard_map/pallas_call | solution.py:368
  227.9 0.0 copy-start.3
  227.9 1.7 fusion.31
  229.6 0.1 copy-done.3
  229.6 0.5 convolution_add_fusion.2
  230.1 0.5 convolution_add_fusion.1
  230.6 0.5 convolution_add_fusion
  231.1 0.0 all-to-all-done.2
  231.1 1.5 slice_convert_fusion
  232.6 1.6 add_reduce_fusion
  234.3 175.1 %fusion.x_ref = f32[1024,512]{1,0:T(8,128)} fusion(f32[1544]{0:T(1024)S(1)} %pad_maximum_fusion.1, s32[1544]{0:T(1024)S(1)} %pad_add_fusion, f32[8,512]{1,0:T(8,128)S(1)} %copy-done.11, f32[1024,512]{1,0:T(8,128)S(1)} %slice_convert_fusion, f32[512,512]{1,0:T(8,128)S(1)} %convolution_add_fusion), kind=kOutput, calls=%fused_computation | convolution fusion | flops 9718751232 | bytes 5271616 | tf_op jit(solution)/shard_map/while/body/eval_jaxpr/dot_general | solution.py:523
  409.3 53.6 %shard_map.95 = f32[1024,512]{1,0:T(8,128)} custom-call(f32[1024,512]{1,0:T(8,128)} %fusion.x_ref), custom_call_target="tpu_custom_call" | custom-call | flops 1048576 | bytes 8388608 | tf_op jit(solution)/shard_map/pallas_call | solution.py:167
  463.0 3.2 copy.84
  466.2 2.0 copy.85
  (27 shorter events, 0.2 us)
Async XLA Ops:
  7.2 1.2 copy-start
  7.2 85.9 %all-gather.2.cloned.1.call-start = ((), (), s32[]{:S(2)}) async-start(), calls=%async_computation.3 | async-start | bytes 2129920 | tf_op jit(solution)/shard_map/all_gather | solution.py:424
  40.6 5.7 %copy-start.10 = (s32[32]{0:T(128)S(1)}, s32[32]{0:T(128)}, u32[]{:S(2)}) copy-start(s32[32]{0:T(128)} %param.13) | copy-start | bytes 388
  40.6 5.8 %copy-start.8 = (s32[512]{0:T(512)S(1)}, s32[512]{0:T(512)}, u32[]{:S(2)}) copy-start(s32[512]{0:T(512)} %param.10) | copy-start | bytes 6148
  40.6 5.8 %copy-start.7 = (s32[512,1]{0,1:T(1,128)S(1)}, s32[512,1]{0,1:T(1,128)}, u32[]{:S(2)}) copy-start(s32[512,1]{0,1:T(1,128)} %param.11) | copy-start | bytes 6148
  40.6 5.8 %copy-start.9 = (s32[512]{0:T(512)S(1)}, s32[512]{0:T(512)}, u32[]{:S(2)}) copy-start(s32[512]{0:T(512)} %param.9) | copy-start | bytes 6148
  40.6 35.3 %all-to-all-start.1 = ((bf16[64,16,512]{2,1,0:T(8,128)(2,1)}), bf16[64,16,512]{2,1,0:T(8,128)(2,1)}, u32[]{:S(2)}, u32[]{:S(2)}) async-start(bf16[64,16,512]{2,1,0:T(8,128)(2,1)} %bitcast.10), calls=%async_computation.1 | async-start | bytes 2097152 | tf_op jit(solution)/shard_map/all_to_all | solution.py:421
  46.2 1.6 copy-start.2
  47.1 2.2 copy-start.4
  102.8 128.3 %all-to-all-start.2 = ((bf16[64,16,640]{2,1,0:T(8,128)(2,1)}), bf16[64,16,640]{2,1,0:T(8,128)(2,1)}, u32[]{:S(2)}, u32[]{:S(2)}) async-start(bf16[64,16,640]{2,1,0:T(8,128)(2,1)} %bitcast.15), calls=%async_computation.2 | async-start | bytes 2621440 | tf_op jit(solution)/shard_map/all_to_all | solution.py:487
  110.6 3.6 copy-start.5
  116.5 2.5 copy-start.1
  227.9 1.8 copy-start.3
  231.1 3.1 copy-start.11
  462.9 3.2 copy-start.6
Sparse Core Ops, SparseCore 0:
  10.8 82.2 all-gather.1

commit v7 on v4

--- a/solution.py
+++ b/solution.py
@@ -513,13 +513,19 @@
     block_rows = ent_dev
     block_count = ent_dev // block_rows
 
+    rows_hi = lax.reduce_precision(target_rows, exponent_bits=8, mantissa_bits=7)
+    rows_rest = target_rows - rows_hi
+    rows_mid = lax.reduce_precision(rows_rest, exponent_bits=8, mantissa_bits=7)
+    rows_split = jnp.concatenate([rows_hi, rows_mid, rows_rest - rows_mid], axis=1).astype(
+        jnp.bfloat16
+    )
+
     def add_block(start):
         hot = (
             target_ids[None, :] == (start + jnp.arange(block_rows, dtype=jnp.int32))[:, None]
-        ).astype(jnp.float32)
-        return jnp.dot(
-            hot, target_rows, precision=lax.Precision.HIGHEST, preferred_element_type=jnp.float32
-        )
+        ).astype(jnp.bfloat16)
+        parts = jnp.dot(hot, rows_split, preferred_element_type=jnp.float32)
+        return (parts[:, :columns] + parts[:, columns : 2 * columns]) + parts[:, 2 * columns :]
 
     local_grad = lax.map(add_block, jnp.arange(block_count, dtype=jnp.int32) * block_rows).reshape(
         ent_dev, columns

time: 308 us -> 310 us (level)
    unnamed x26 -> x30, local copies, waits for them, and re-layouts: 7.21 us -> 7.22 us
  transfers between devices with their start and end apart: 3 -> 3, of which waited for: 2 -> 2; matrix products, arithmetic and copies ran while one was open for 10% -> 9% of each run, Pallas kernels for 34% -> 34%
where the time goes in v7:
time: 310 us
  Pallas kernels  159 us (51%)
  waiting for transfers between devices  41.2 us (13%)
  matrix products  30.9 us (10%)
  blocking collectives  22.1 us (7%)
  other arithmetic  15.8 us (5%)
  between operations  14.4 us (5%)
  starting transfers between devices  13.4 us (4%)
  local copies, waits for them, and re-layouts  12.5 us (4%)
    pallas_call x1, Pallas kernels, lane_reduce(): pl.pallas_call(functools.partial(_lane_kernel, tuple(lanes), (n_dom, n_re...  106 us
    pallas_call x1, Pallas kernels, tree_reduce(): pl.pallas_call(functools.partial(_reduce_kernel, tuple(rs), tuple(ag), (n...  53.7 us
    all_to_all x1, waiting for transfers between devices, local(): lax.all_to_all(looked_up, 'dom', split_axis=0, concat_axis=0, tiled=True)  25.4 us
    all_to_all x1, blocking collectives, local(): lax.all_to_all(send_ids, 'dom', split_axis=0, concat_axis=0, tiled=True)  22.1 us
    all_gather x1, waiting for transfers between devices, local(): negatives = lax.all_gather(own_negs, 'dom', axis=0, tiled=True)  15.7 us
    all_to_all x1, starting transfers between devices, local(): lax.all_to_all(pack_send.reshape(part_count, capacity, pack.shape[1]), 'd...  7.68 us
    dot_general x4, matrix products, pick_rows(): jnp.dot(hot, table, preferred_element_type=jnp.float32).astype(table.dtype)  7.41 us
    unnamed x30, local copies, waits for them, and re-layouts  7.22 us
  transfers between devices with their start and end apart: 3, of which 2 were waited for; matrix products, arithmetic and copies ran while one was open for 9% of the time, Pallas kernels for 34%

profile of v7, /device:TPU:1, one launch (start us, length us, event | category | flops | bytes accessed | tf_op | source)
XLA Modules:
  0.0 309.6 jit_solution(4166412116459201234)
XLA Ops:
  7.2 0.0 copy-start
  7.2 0.0 all-gather.2.cloned.1.call-start
  7.2 1.2 copy-done
  8.4 1.6 convolution_convert_fusion.1
  10.0 0.0 all-gather.2.cloned.1.call-update
  10.0 0.7 fusion.56
  10.7 1.2 reduce-window.6
  11.9 0.2 slice_reduce_fusion
  12.2 0.8 fusion.55
  13.0 0.7 multiply_add_fusion.1
  13.7 1.0 select_reduce_fusion
  14.7 0.1 all_to_all.12
  14.7 22.1 %all_to_all.19 = s32[64,1,16]{2,1,0:T(1,128)S(1)} all-to-all(s32[64,1,16]{2,1,0:T(1,128)S(1)} %bitcast.85), channel_id=1, replica_groups=mesh['dom'=64,'rep'=4] {'dom'}, dimensions={0} | all-to-all | bytes 8192 | tf_op jit(solution)/shard_map/all_to_all | solution.py:417
  36.9 0.5 broadcast.166
  37.4 0.7 reduce.7
  38.1 0.1 reshape.167
  38.2 2.3 fusion.13
  40.5 5.7 %all-to-all-start.1 = ((bf16[64,16,512]{2,1,0:T(8,128)(2,1)}), bf16[64,16,512]{2,1,0:T(8,128)(2,1)}, u32[]{:S(2)}, u32[]{:S(2)}) async-start(bf16[64,16,512]{2,1,0:T(8,128)(2,1)} %bitcast.10), calls=%async_computation.1 | async-start | bytes 2097152 | tf_op jit(solution)/shard_map/all_to_all | solution.py:421
  46.2 0.0 copy-start.2
  46.2 0.0 copy-done.13
  46.2 0.1 dynamic_slice.6
  46.3 0.8 fusion.17
  47.1 0.7 copy-done.2
  47.8 0.5 fusion.31
  48.3 0.5 convolution_add_fusion.5
  48.8 0.5 convolution_add_fusion.4
  49.3 0.5 fusion.18
  49.8 25.4 %all-to-all-done.1 = bf16[64,16,512]{2,1,0:T(8,128)(2,1)} async-done(((bf16[64,16,512]{2,1,0:T(8,128)(2,1)}), bf16[64,16,512]{2,1,0:T(8,128)(2,1)}, u32[]{:S(2)}, u32[]{:S(2)}) %all-to-all-start.1) | async-done | bytes 1048608 | tf_op jit(solution)/shard_map/all_to_all | solution.py:421
  75.2 2.8 fusion.19
  78.0 15.7 %all-gather.2.cloned.1.call-done = bf16[2048,512]{1,0:T(8,128)(2,1)} async-done(((bf16[32,512]{1,0:T(8,128)(2,1)}), bf16[2048,512]{1,0:T(8,128)(2,1)}) %all-gather.2.cloned.1.call-update) | async-done | bytes 2097168 | tf_op jit(solution)/shard_map/all_gather | solution.py:424
  93.7 3.0 multiply_reduce_fusion
  96.7 0.8 fusion.7
  97.5 0.6 add_subtract_fusion
  98.1 0.8 divide_convert_fusion
  99.0 0.2 copy.72
  99.2 0.2 copy.73
  99.4 0.2 copy.74
  99.6 1.1 concatenate.15
  100.7 3.1 %convolution_convert_fusion = bf16[1024,640]{1,0:T(8,128)(2,1)} fusion(bf16[512,640]{1,0:T(8,128)(2,1)} %concatenate.15, s32[512]{0:T(512)S(1)} %multiply_add_fusion.1), kind=kOutput, calls=%fused_computation.33 | convolution fusion | flops 673316864 | bytes 1968128 | tf_op jit(solution)/shard_map/dot_general | solution.py:484
  103.9 7.7 %all-to-all-start.2 = ((bf16[64,16,640]{2,1,0:T(8,128)(2,1)}), bf16[64,16,640]{2,1,0:T(8,128)(2,1)}, u32[]{:S(2)}, u32[]{:S(2)}) async-start(bf16[64,16,640]{2,1,0:T(8,128)(2,1)} %bitcast.84), calls=%async_computation.2 | async-start | bytes 2621440 | tf_op jit(solution)/shard_map/all_to_all | solution.py:487
  111.6 3.0 fusion.15
  114.6 0.6 convolution_bitcast_fusion
  115.1 0.6 convolution_bitcast_fusion.1
  115.7 0.6 convolution_bitcast_fusion.2
  116.3 0.6 convolution_bitcast_fusion.3
  116.8 2.5 pad_maximum_fusion
  119.3 1.3 convolution_multiply_fusion
  120.6 2.6 copy.75
  123.2 105.6 %shard_map.94 = (f32[2048,512]{1,0:T(8,128)}, f32[8,512]{1,0:T(8,128)}) custom-call(f32[2048,512]{1,0:T(8,128)} %bitcast.81, f32[2048,512]{1,0:T(8,128)} %bitcast.82), custom_call_target="tpu_custom_call" | custom-call | flops 8388608 | bytes 33554432 | tf_op jit(solution)/shard_map/pallas_call | solution.py:368
  228.8 0.0 copy-start.3
  228.8 1.7 fusion.29
  230.5 0.1 copy-done.3
  230.6 0.5 convolution_add_fusion.2
  231.1 0.5 convolution_add_fusion.1
  231.5 0.5 convolution_add_fusion
  232.1 0.0 all-to-all-done.2
  232.1 1.6 add_reduce_fusion
  233.6 1.4 convert_multiply_fusion
  235.1 0.8 reduce-precision_convert_fusion.1
  235.9 5.8 %fusion = f32[1024,1536]{1,0:T(8,128)S(1)} fusion(bf16[1544,512]{1,0:T(8,128)(2,1)S(1)} %get-tuple-element.29, bf16[1544,512]{1,0:T(8,128)(2,1)S(1)} %get-tuple-element.28, bf16[1544,512]{1,0:T(8,128)(2,1)S(1)} %get-tuple-element.27, s32[1544]{0:T(1024)S(1)} %pad_add_fusion), kind=kOutput, calls=%fused_computation.1 | convolution fusion | flops 4872814592 | bytes 11040800 | tf_op jit(solution)/shard_map/while/body/eval_jaxpr/dot_general | solution.py:527
  241.7 2.1 slice_add_fusion.x_ref
  243.8 53.7 %shard_map.95 = f32[1024,512]{1,0:T(8,128)} custom-call(f32[1024,512]{1,0:T(8,128)} %slice_add_fusion.x_ref), custom_call_target="tpu_custom_call" | custom-call | flops 1048576 | bytes 8388608 | tf_op jit(solution)/shard_map/pallas_call | solution.py:167
  297.5 3.2 %copy.85 = f32[1024,512]{1,0:T(8,128)} copy(f32[1024,512]{1,0:T(8,128)} %shard_map.95) | data formatting | bytes 4194304
  300.7 2.0 copy.86
  (30 shorter events, 0.2 us)
Async XLA Ops:
  7.2 1.2 copy-start
  7.2 86.6 %all-gather.2.cloned.1.call-start = ((), (), s32[]{:S(2)}) async-start(), calls=%async_computation.3 | async-start | bytes 2129920 | tf_op jit(solution)/shard_map/all_gather | solution.py:424
  40.5 5.7 %copy-start.13 = (s32[32]{0:T(128)S(1)}, s32[32]{0:T(128)}, u32[]{:S(2)}) copy-start(s32[32]{0:T(128)} %param.13) | copy-start | bytes 388
  40.5 5.8 %copy-start.11 = (s32[512]{0:T(512)S(1)}, s32[512]{0:T(512)}, u32[]{:S(2)}) copy-start(s32[512]{0:T(512)} %param.10) | copy-start | bytes 6148
  40.5 5.8 %copy-start.9 = (s32[512,1]{0,1:T(1,128)S(1)}, s32[512,1]{0,1:T(1,128)}, u32[]{:S(2)}) copy-start(s32[512,1]{0,1:T(1,128)} %param.11) | copy-start | bytes 6148
  40.5 5.8 %copy-start.12 = (s32[512]{0:T(512)S(1)}, s32[512]{0:T(512)}, u32[]{:S(2)}) copy-start(s32[512]{0:T(512)} %param.9) | copy-start | bytes 6148
  40.5 34.7 %all-to-all-start.1 = ((bf16[64,16,512]{2,1,0:T(8,128)(2,1)}), bf16[64,16,512]{2,1,0:T(8,128)(2,1)}, u32[]{:S(2)}, u32[]{:S(2)}) async-start(bf16[64,16,512]{2,1,0:T(8,128)(2,1)} %bitcast.10), calls=%async_computation.1 | async-start | bytes 2097152 | tf_op jit(solution)/shard_map/all_to_all | solution.py:421
  46.2 1.6 copy-start.2
  47.1 2.2 copy-start.4
  103.9 128.2 %all-to-all-start.2 = ((bf16[64,16,640]{2,1,0:T(8,128)(2,1)}), bf16[64,16,640]{2,1,0:T(8,128)(2,1)}, u32[]{:S(2)}, u32[]{:S(2)}) async-start(bf16[64,16,640]{2,1,0:T(8,128)(2,1)} %bitcast.84), calls=%async_computation.2 | async-start | bytes 2621440 | tf_op jit(solution)/shard_map/all_to_all | solution.py:487
  111.5 3.0 copy-start.5
  114.6 1.7 copy-start.6
  123.2 105.6 %copy-start.7 = (bf16[512,512]{1,0:T(8,128)(2,1)S(1)}, bf16[512,512]{1,0:T(8,128)(2,1)}, u32[]{:S(2)}) copy-start(bf16[512,512]{1,0:T(8,128)(2,1)} %copy-done.6) | copy-start | bytes 1572868
  228.8 1.8 copy-start.3
  232.0 3.0 copy-start.10
  297.5 3.2 %copy-start.8 = (f32[2048,512]{1,0:T(8,128)S(1)}, f32[2048,512]{1,0:T(8,128)}, u32[]{:S(2)}) copy-start(f32[2048,512]{1,0:T(8,128)} %get-tuple-element.24) | copy-start | bytes 12582916
  300.7 2.0 copy-start.1
Sparse Core Ops, SparseCore 0:
  11.4 82.3 all-gather.1
